TPU v7x, 256 devices: a whole 4x4x8 slice. The times are simulated.
256 devices in a mesh: dp: 4 (over y_hi, core), bank: 64 (over y_lo, x, z).
Axes of the slice: x: 4, y: 4 (y_hi: 2, y_lo: 2; y = y_hi * 2 + y_lo), z: 8, core: 2. Of those that a mesh axis runs over, the one named last changes fastest.
Arguments:
- features: bfloat16 [64, 4096, 256], P('dp', 'bank'), may hold values from -6 to 6
- patch_index: int32 [64, 128], P('dp'), may hold values from 0 to 4095, as said below
- positive_index: int32 [8192], P('dp'), may hold values from 0 to 262143
- bank: bfloat16 [262144, 256], P('bank'), may hold values from -0.4 to 0.4
Outputs:
- loss: float32 [8192], P(('dp', 'bank'))
- query_grad: float32 [8192, 256], P(('dp', 'bank'))
- mean_loss: float32 [], replicated
Inputs may be any that keep to these rules, and one draw needn't show every extreme that they name: `patch_index`: within one image the sampled positions are distinct.
All inputs are finite; a program needn't handle non-finite values.
Results may differ from a plain program's by a relative error of at most 0.00065.
Values may be sent and summed in bfloat16 or wider, within the bound.
A program may use at most 64 MiB of HBM per device.

v0:
```python
import math

import jax
import jax.numpy as jnp
from jax import lax
from jax.sharding import PartitionSpec as P

SOFTMAX_TEMP = 0.07
EPSILON = 1e-05


def normalize(values):
    scale = lax.rsqrt(jnp.mean(values * values, axis=-1, keepdims=True) + EPSILON)
    return values * scale / math.sqrt(values.shape[-1])


def on_device(features, patch_index, positive_index, bank):
    groups = lax.axis_size("bank")
    place = lax.axis_index("bank")
    images, hw_dev, channels = features.shape
    queries_dp = images * patch_index.shape[1]
    owned_rows = queries_dp // groups
    local_pos = patch_index - place * hw_dev
    onehot = (local_pos[:, :, None] == jnp.arange(hw_dev, dtype=jnp.int32)[None, None, :]).astype(
        jnp.bfloat16
    )
    picked = jnp.einsum("iph,ihc->ipc", onehot, features, preferred_element_type=jnp.float32)
    term = picked.reshape(queries_dp, channels)
    raw_all = lax.psum(term, "bank")
    query_vector = normalize(raw_all).astype(jnp.bfloat16)
    raw_own = lax.dynamic_slice_in_dim(raw_all, place * owned_rows, owned_rows, 0)
    bank_dev = bank.shape[0]
    block_keys = math.gcd(bank_dev, 512)

    def visit(index, carry):
        exponent_sum, weighted_negatives = carry
        bank_block = lax.dynamic_slice_in_dim(bank, index * block_keys, block_keys, 0)
        logit_scores = (
            lax.dot_general(
                query_vector,
                bank_block,
                (((1,), (1,)), ((), ())),
                preferred_element_type=jnp.float32,
            )
            / SOFTMAX_TEMP
        )
        exponent_terms = jnp.exp(logit_scores - 1.0 / SOFTMAX_TEMP)
        exponent_sum = exponent_sum + jnp.sum(exponent_terms, axis=1)
        weighted_negatives = weighted_negatives + jnp.dot(
            exponent_terms.astype(jnp.bfloat16), bank_block, preferred_element_type=jnp.float32
        )
        return (exponent_sum, weighted_negatives)

    start = (jnp.zeros((queries_dp,), jnp.float32), jnp.zeros((queries_dp, channels), jnp.float32))
    exponent_sum, weighted_negatives = lax.fori_loop(0, bank_dev // block_keys, visit, start)
    key_pos = positive_index - place * bank_dev
    inside = (key_pos >= 0) & (key_pos < bank_dev)
    rows_pos = jnp.clip(key_pos, 0, bank_dev - 1)
    positive_key = bank[rows_pos].astype(jnp.float32) * inside[:, None].astype(jnp.float32)
    matched_logit = jnp.sum(query_vector.astype(jnp.float32) * positive_key, axis=1) / SOFTMAX_TEMP
    local_exponent_sum, local_logit, local_weighted, local_positive = (
        lax.psum_scatter(exponent_sum, "bank", scatter_dimension=0, tiled=True),
        lax.psum_scatter(matched_logit, "bank", scatter_dimension=0, tiled=True),
        lax.psum_scatter(weighted_negatives, "bank", scatter_dimension=0, tiled=True),
        lax.psum_scatter(positive_key, "bank", scatter_dimension=0, tiled=True),
    )
    query_update = (local_weighted / local_exponent_sum[:, None] - local_positive) / SOFTMAX_TEMP
    loss = jnp.log(local_exponent_sum) + 1.0 / SOFTMAX_TEMP - local_logit
    _, pullback = jax.vjp(normalize, raw_own)
    query_grad = pullback(query_update)[0]
    count_all = queries_dp * lax.axis_size("dp")
    mean_loss = lax.psum(jnp.sum(loss), ("dp", "bank")) / count_all
    return (loss, query_grad, mean_loss)


def solution(mesh):
    in_specs = (P("dp", "bank", None), P("dp", None), P("dp"), P("bank", None))
    out_specs = (P(("dp", "bank")), P(("dp", "bank"), None), P())
    return jax.shard_map(
        on_device, mesh=mesh, in_specs=in_specs, out_specs=out_specs, check_vma=False
    )
```

profile of v0, /device:TPU:16, one launch (start us, length us, event | category | flops | bytes accessed | tf_op | source)
XLA Modules:
  0.0 1278.5 jit_solution(1991647624746755752)
XLA Ops:
  7.2 0.0 copy-start
  7.2 0.0 all-reduce.5.cloned.1.call-start
  7.2 0.7 broadcast_subtract_fusion
  8.0 0.2 copy-done
  8.2 0.0 copy-start.3
  8.2 1.8 fusion.12
  10.0 0.0 all-reduce.5.cloned.1.call-update
  10.0 0.0 reduce-scatter.5.cloned.1.call-start
  10.1 0.0 copy-done.3
  10.1 10.3 gather_fusion
  20.5 606.7 %all-reduce.5.cloned.1.call-done = f32[2048,256]{1,0:T(8,128)} async-done(((f32[2048,256]{1,0:T(8,128)}), f32[2048,256]{1,0:T(8,128)}) %all-reduce.5.cloned.1.call-update) | async-done | bytes 2097168 | tf_op jit(solution)/shard_map/psum | solution.py:29
  627.1 0.0 copy-start.2
  627.1 2.1 multiply_reduce_fusion.1
  629.3 0.1 copy-done.2
  629.4 3.2 multiply_reduce_fusion
  632.5 0.0 reduce-scatter.5.cloned.1.call-update
  632.6 0.0 reduce-scatter.3.cloned.1.call-start
  632.6 42.5 %while.18 = (s32[]{:T(128)}, f32[2048]{0:T(1024)S(1)}, f32[2048,256]{1,0:T(8,128)S(1)}, bf16[4096,256]{1,0:T(8,128)(2,1)}, bf16[2048,256]{1,0:T(8,128)(2,1)}, /*index=5*/s32[]{:T(128)}, s32[]{:T(128)}, s32[]{:T(128)}, s32[]{:T(128)}) while((s32[]{:T(128)}, f32[2048]{0:T(1024)S(1)}, f32[2048,256]{1,0:T(8,128)S(1)}, ...), condition=%wide.region_4.0_spmd.clone, body=%wide.region_2.0_spmd.clone.sunk | while | flops 1081083904 | bytes 14188710 | solution.py:55
  632.6 2.4 fusion.28
  635.1 2.8 convolution_add_fusion.2
  637.9 2.4 fusion.28
  640.4 2.8 convolution_add_fusion.2
  643.3 2.4 fusion.28
  645.7 2.8 convolution_add_fusion.2
  648.6 2.4 fusion.28
  651.0 2.8 convolution_add_fusion.2
  653.9 2.4 fusion.28
  656.4 2.8 convolution_add_fusion.2
  659.2 2.4 fusion.28
  661.7 2.8 convolution_add_fusion.2
  664.5 2.4 fusion.28
  667.0 2.8 convolution_add_fusion.2
  669.8 2.4 fusion.28
  672.3 2.8 convolution_add_fusion.2
  675.2 0.0 copy-start.1
  675.2 0.0 copy-start.4
  675.2 1.3 copy-done.1
  676.5 0.0 reduce-scatter.3.cloned.1.call-update
  676.5 0.0 copy-done.4
  676.5 0.6 dynamic-slice
  677.8 307.7 %all-reduce.2 = (f32[2048]{0:T(1024)S(1)}, f32[2048]{0:T(1024)S(1)}) all-reduce(f32[2048]{0:T(1024)S(1)} %broadcast_multiply_fusion, f32[2048]{0:T(1024)S(1)} %get-tuple-element.136), channel_id=3, replica_groups=mesh['dp'=4,'bank'=64] {'bank'}, use_global_device_ids=true, to_apply=%region_7.8.clone | all-reduce | flops 4096 | bytes 32768
  985.5 1.2 fusion.18
  986.7 72.9 %psum.15 = f32[]{:T(128)} all-reduce(f32[]{:T(128)} %get-tuple-element.170), channel_id=1, replica_groups=mesh['dp'=4,'bank'=64] {'dp','bank'}, use_global_device_ids=true, to_apply=%region_13.14 | all-reduce | flops 1 | bytes 8 | tf_op jit(solution)/shard_map/psum | solution.py:72
  1060.3 0.0 reduce-scatter.5.cloned.1.call-done
  1060.3 208.0 %reduce-scatter.3.cloned.1.call-done = f32[32,256]{1,0:T(8,128)} async-done(((f32[2048,256]{1,0:T(8,128)}), f32[32,256]{1,0:T(8,128)}) %reduce-scatter.3.cloned.1.call-update) | async-done | bytes 32784 | tf_op jit(solution)/shard_map/reduce_scatter | solution.py:64
  1268.3 1.0 multiply_reduce_fusion.3
  1269.3 1.5 add_add_fusion
  (15 shorter events, 0.1 us)
Async XLA Ops:
  7.2 1.1 copy-start
  7.2 620.0 %all-reduce.5.cloned.1.call-start = ((), (), s32[]{:S(2)}) async-start(), calls=%async_computation.2 | async-start | bytes 4194304 | tf_op jit(solution)/shard_map/psum | solution.py:29
  8.2 1.9 copy-start.3
  10.0 1050.2 %reduce-scatter.5.cloned.1.call-start = ((), (), s32[]{:S(2)}) async-start(), calls=%async_computation.4 | async-start | bytes 2129920 | tf_op jit(solution)/shard_map/reduce_scatter | solution.py:65
  627.1 2.2 copy-start.2
  632.6 635.8 %reduce-scatter.3.cloned.1.call-start = ((), (), s32[]{:S(2)}) async-start(), calls=%async_computation.3 | async-start | bytes 2129920 | tf_op jit(solution)/shard_map/reduce_scatter | solution.py:64
  675.2 1.3 copy-start.1
  675.2 1.4 copy-start.4
Sparse Core Ops, SparseCore 0:
  10.6 616.5 all-reduce.4
  632.7 318.3 reduce-scatter.4
  953.6 314.7 reduce-scatter.2
where the time goes:
time: 1280 us
  waiting for transfers between devices  815 us (64%)
  blocking collectives  381 us (30%)
  matrix products  43.9 us (3%)
  between operations  16.3 us (1%)
    psum x1, waiting for transfers between devices, on_device(): raw_all = lax.psum(term, 'bank')  607 us
    unnamed x1, blocking collectives  308 us
    reduce_scatter x1, waiting for transfers between devices, on_device(): lax.psum_scatter(weighted_negatives, 'bank', scatter_dimension=0, tiled=T...  208 us
    psum x1, blocking collectives, on_device(): mean_loss = lax.psum(jnp.sum(loss), ('dp', 'bank')) / count_all  72.9 us
  transfers between devices with their start and end apart: 3, of which 2 were waited for; matrix products, arithmetic and copies ran while one was open for 4% of the time, Pallas kernels for 0%

commit v1 on v0

v1 whole, which is shorter than its diff:
```python
import itertools
import math

import jax
import jax.numpy as jnp
from jax import lax
from jax.experimental import pallas as pl
from jax.experimental.pallas import tpu as pltpu
from jax.sharding import PartitionSpec as P

SOFTMAX_TEMP = 0.07
EPSILON = 1e-05
MESH = pl.DeviceIdType.MESH
F32, BF16 = jnp.float32, jnp.bfloat16

NY, NX, NZ = 2, 4, 8
ROWS = 32
HALF = NZ * ROWS
N_SEMS = 96


def bank_id(y, x, z):
    return (y * NX + x) * NZ + z


def kernel(
    count_all,
    patch_ref,
    pos_ref,
    feat_ref,
    bank_ref,
    loss_ref,
    grad_ref,
    mean_ref,
    fb, fa, fu, fm, fc, fs, fz, fy,
    pb, pa, pu, pm, pc, ps, pz, py,
    qa, raw,
    wf, wb, wa, wu, wm, wc, ws, wo, wz, wys, wy,
    acc, tacc,
    ts, tx, t2, tz, t3, ty, tt,
    ms, mx, mz, my,
    col,
    ssem, rsem,
):
    place, dp = lax.axis_index("bank"), lax.axis_index("dp")
    y, x, z = place // (NX * NZ), (place // NZ) % NX, place % NZ
    corner = (dp // 2) * 4 + y * 2 + dp % 2
    xp, xo, xm = (x + 1) % NX, (x + 2) % NX, (x + 3) % NX
    x_peers = [{"bank": bank_id(y, (x + k) % NX, z)} for k in range(1, NX)]
    z_at = [(z + k) % NZ for k in range(1, NZ)]
    z_peers = [{"bank": bank_id(y, x, at)} for at in z_at]
    y_peer = {"bank": bank_id(1 - y, x, z)}
    c_peers = []
    for k in range(1, 8):
        other = (corner + k) % 8
        c_peers.append(
            {"dp": (other // 4) * 2 + other % 2, "bank": bank_id((other // 2) % 2, x, z)}
        )
    plus, minus = x_peers[0], x_peers[2]
    count = itertools.count()

    def remote(src, dst, peer):
        i = next(count)
        return pltpu.make_async_remote_copy(
            src_ref=src,
            dst_ref=dst,
            send_sem=ssem.at[i],
            recv_sem=rsem.at[i],
            device_id=peer,
            device_id_type=MESH,
        )

    started = []

    def go(copies):
        for copy in copies:
            copy.start()
            started.append(copy)

    barrier = pltpu.get_barrier_semaphore()
    greeted = x_peers + z_peers + c_peers
    for peer in greeted:
        pl.semaphore_signal(barrier, inc=1, device_id=peer, device_id_type=MESH)

    images, spots, channels = feat_ref.shape
    patches = patch_ref.shape[0]
    for i in range(images):
        hit = patch_ref[:, i : i + 1] == lax.broadcasted_iota(jnp.int32, (patches, spots), 1)
        picked = jnp.dot(hit.astype(BF16), feat_ref[i], preferred_element_type=F32)
        first = i * patches
        fb[first // HALF % NX, first // (HALF * NX), pl.ds(first % HALF, patches), :] = (
            picked.astype(BF16)
        )
    pl.semaphore_wait(barrier, len(greeted))

    def x_first(b, a, u):
        return [
            remote(b.at[xo, 0], a.at[0], plus),
            remote(b.at[xo, 1], a.at[1], minus),
            remote(b.at[xp, 1], u.at[1], plus),
            remote(b.at[xm, 0], u.at[0], minus),
        ]

    def x_second(m, c):
        return [remote(m.at[0], c.at[0], plus), remote(m.at[1], c.at[1], minus)]

    def z_send(s, r):
        return [
            remote(s.at[:, at], r.at[k], peer) for k, (at, peer) in enumerate(zip(z_at, z_peers))
        ]

    def merge_exact(b, a, m, first, second):
        first[0].wait_recv()
        m[0] = a[0] + b[xp, 0]
        go(second[:1])
        first[1].wait_recv()
        m[1] = a[1] + b[xm, 1]
        go(second[1:])

    def x_total_exact(b, u, c, s, first, second):
        first[2].wait_recv()
        first[3].wait_recv()
        second[0].wait_recv()
        second[1].wait_recv()
        for h in range(NY):
            s[h] = (b[x, h] + u[h] + c[h]).reshape(NZ, ROWS, channels)

    def z_total_exact(s, r, copies):
        total = s[:, z]
        for k, copy in enumerate(copies):
            copy.wait_recv()
            total = total + r[k]
        return total

    f1, f2 = x_first(fb, fa, fu), x_second(fm, fc)
    go(f1)

    bank_dev = bank_ref.shape[0]
    for g in range(pos_ref.shape[1]):
        col[pl.ds(g * 128, 128), :] = pos_ref[:, g : g + 1]
    wide = 1024

    def take(block, carry):
        rows = col[pl.ds(pl.multiple_of(block * HALF, HALF), HALF), :]

        def part(j, _):
            start = pl.multiple_of(j * wide, wide)
            keys = lax.broadcasted_iota(jnp.int32, (HALF, wide), 1) + start
            one = jnp.where(rows == keys, 1.0, 0.0).astype(BF16)
            got = jnp.dot(one, bank_ref[pl.ds(start, wide), :], preferred_element_type=F32)
            acc[...] = acc[...] + got
            return 0

        acc[...] = jnp.zeros_like(acc)
        lax.fori_loop(0, bank_dev // wide, part, 0)
        pb[block % NX, block // NX] = acc[...].astype(BF16)
        return carry

    lax.fori_loop(0, NX * NY, take, 0)

    merge_exact(fb, fa, fm, f1, f2)
    x_total_exact(fb, fu, fc, fs, f1, f2)
    f3 = z_send(fs, fz)
    go(f3)
    p1, p2 = x_first(pb, pa, pu), x_second(pm, pc)
    go(p1)
    fs[:, z] = z_total_exact(fs, fz, f3)
    f4 = remote(fs.at[1 - y, z], fy, y_peer)
    go([f4])
    f4.wait_recv()
    own = (fs[y, z] + fy[...]).astype(F32)
    raw[...] = own
    scale = lax.rsqrt(jnp.mean(own * own, axis=-1, keepdims=True) + EPSILON)
    qa[x, y, z] = (own * scale / math.sqrt(channels)).astype(BF16)

    g1 = remote(qa.at[x, y, z], qa.at[x, y, z], y_peer)
    go([g1])
    merge_exact(pb, pa, pm, p1, p2)
    g1.wait_recv()
    g2 = [remote(qa.at[x, :, z], qa.at[x, :, z], peer) for peer in z_peers]
    go(g2)
    x_total_exact(pb, pu, pc, ps, p1, p2)
    for copy in g2:
        copy.wait_recv()
    g3 = [
        remote(qa.at[x, 0], qa.at[x, 0], plus),
        remote(qa.at[x, 1], qa.at[x, 1], minus),
        remote(qa.at[x, 1], qa.at[x, 1], plus),
        remote(qa.at[x, 0], qa.at[x, 0], minus),
    ]
    g4 = [
        remote(qa.at[xm, 0], qa.at[xm, 0], plus),
        remote(qa.at[xp, 1], qa.at[xp, 1], minus),
    ]
    go(g3)
    p3 = z_send(ps, pz)
    go(p3)

    factor = 1.0 / (SOFTMAX_TEMP * math.log(2.0))
    block_keys = 2048

    def unit(at, h):
        query = qa[at, h].reshape(HALF, channels)
        acc[...] = jnp.zeros_like(acc)
        tacc[...] = jnp.zeros_like(tacc)

        def step(j, _):
            keys = bank_ref[pl.ds(pl.multiple_of(j * block_keys, block_keys), block_keys), :]
            dots = lax.dot_general(
                query, keys, (((1,), (1,)), ((), ())), preferred_element_type=F32
            )
            terms = jnp.exp2(dots * factor - factor)
            some = terms[:, :128]
            for lane in range(128, block_keys, 128):
                some = some + terms[:, lane : lane + 128]
            tacc[...] = tacc[...] + some
            acc[...] = acc[...] + jnp.dot(terms.astype(BF16), keys, preferred_element_type=F32)
            return 0

        lax.fori_loop(0, bank_dev // block_keys, step, 0)
        sums = jnp.sum(jnp.transpose(tacc[...]), axis=0, keepdims=True)
        ts[at, pl.ds(2 * h, 1), :] = sums[:, :128]
        ts[at, pl.ds(2 * h + 1, 1), :] = sums[:, 128:]

    ts[...] = jnp.zeros_like(ts)
    unit(x, 0)
    wf[0] = acc[...]
    g3[0].wait_recv()
    g3[1].wait_recv()
    go(g4)
    unit(x, 1)
    wf[1] = acc[...]
    w1, w2 = x_first(wb, wa, wu), x_second(wm, wc)

    g3[3].wait_recv()
    unit(xp, 0)
    wf[2] = acc[...]
    unit(xp, 1)
    wb[xp, 1] = acc[...].astype(BF16)
    go(w1[2:3])
    g4[0].wait_recv()
    g4[1].wait_recv()
    unit(xo, 0)
    wb[xo, 0] = acc[...].astype(BF16)
    go(w1[0:1])
    unit(xo, 1)
    wb[xo, 1] = acc[...].astype(BF16)
    go(w1[1:2])
    g3[2].wait_recv()
    unit(xm, 0)
    wb[xm, 0] = acc[...].astype(BF16)
    go(w1[3:4])
    w1[0].wait_recv()
    wm[0] = (wa[0].astype(F32) + wf[2]).astype(BF16)
    go(w2[:1])
    unit(xm, 1)
    t1 = [remote(ts.at[(x + k) % NX], tx.at[k - 1], x_peers[k - 1]) for k in range(1, NX)]
    go(t1)
    w1[1].wait_recv()
    wm[1] = (wa[1].astype(F32) + acc[...]).astype(BF16)
    go(w2[1:])

    ps[:, z] = z_total_exact(ps, pz, p3)
    p4 = remote(ps.at[1 - y, z], py, y_peer)
    go([p4])

    total = ts[x]
    for k, copy in enumerate(t1):
        copy.wait_recv()
        total = total + tx[k]
    t2[...] = total
    t4 = [remote(t2, tz.at[k], peer) for k, peer in enumerate(z_peers)]
    go(t4)

    w1[2].wait_recv()
    w1[3].wait_recv()
    w2[0].wait_recv()
    w2[1].wait_recv()
    for h in range(NY):
        part = wf[h] + wu[h].astype(F32) + wc[h].astype(F32)
        part = part.reshape(NZ, ROWS, channels)
        wo[h] = part
        ws[h] = part.astype(BF16)
    w3 = z_send(ws, wz)
    go(w3)

    total = t2[...]
    for k, copy in enumerate(t4):
        copy.wait_recv()
        total = total + tz[k]
    t3[...] = total
    t5 = remote(t3, ty, y_peer)
    go([t5])
    p4.wait_recv()
    positive = (ps[y, z] + py[...]).astype(F32)
    query = qa[x, y, z].astype(F32)
    matched = jnp.sum(query * positive, axis=1, keepdims=True) / SOFTMAX_TEMP
    t5.wait_recv()
    tt[...] = t3[...] + ty[...]
    line = tt[pl.ds(2 * y + z // 4, 1), :]
    lane = lax.broadcasted_iota(jnp.int32, (ROWS, 128), 1)
    row = lax.broadcasted_iota(jnp.int32, (ROWS, 128), 0)
    mine = jnp.where(lane == row + (z % 4) * ROWS, jnp.broadcast_to(line, (ROWS, 128)), 0.0)
    exponent_sum = jnp.sum(mine, axis=1, keepdims=True)
    loss = jnp.log(exponent_sum) + 1.0 / SOFTMAX_TEMP - matched
    diagonal = lax.broadcasted_iota(jnp.int32, (ROWS, ROWS), 0) == lax.broadcasted_iota(
        jnp.int32, (ROWS, ROWS), 1
    )
    loss_ref[...] = jnp.sum(
        jnp.where(diagonal, jnp.broadcast_to(loss, (ROWS, ROWS)), 0.0), axis=0, keepdims=True
    )

    ms[0] = jnp.broadcast_to(jnp.sum(loss, axis=0, keepdims=True), (8, 128))
    m1 = [remote(ms.at[0], mx.at[k], peer) for k, peer in enumerate(x_peers)]
    go(m1)
    for k, copy in enumerate(m1):
        copy.wait_recv()
    ms[1] = ms[0] + (mx[0] + mx[1] + mx[2])
    m2 = [remote(ms.at[1], mz.at[k], peer) for k, peer in enumerate(z_peers)]
    go(m2)

    part = wo[:, z]
    for k, copy in enumerate(w3):
        copy.wait_recv()
        part = part + wz[k].astype(F32)
    wys[...] = part
    w4 = remote(wys.at[1 - y], wy, y_peer)
    go([w4])

    losses = ms[1]
    for k, copy in enumerate(m2):
        copy.wait_recv()
        losses = losses + mz[k]
    ms[2] = losses
    m3 = [remote(ms.at[2], my.at[k], peer) for k, peer in enumerate(c_peers)]
    go(m3)

    w4.wait_recv()
    weighted = wys[y] + wy[...]
    step = (weighted / exponent_sum - positive) / SOFTMAX_TEMP
    own = raw[...]
    scale = lax.rsqrt(jnp.mean(own * own, axis=-1, keepdims=True) + EPSILON)
    inner = jnp.mean(step * own, axis=-1, keepdims=True)
    grad_ref[...] = (scale / math.sqrt(channels)) * (step - own * (scale * scale * inner))

    losses = ms[2]
    for k, copy in enumerate(m3):
        copy.wait_recv()
        losses = losses + my[k]
    mean_ref[...] = losses[:1] / count_all
    for copy in started:
        copy.wait_send()


def on_device(features, patch_index, positive_index, bank):
    place = lax.axis_index("bank")
    images, hw_dev, channels = features.shape
    patches = patch_index.shape[1]
    queries_dp = images * patches
    spots = jnp.transpose(patch_index) - place * hw_dev
    keys = jnp.transpose(positive_index.reshape(-1, 128)) - place * bank.shape[0]
    count_all = queries_dp * lax.axis_size("dp")

    def vmem(dtype, *shape):
        return pltpu.VMEM(shape, dtype)

    def exact():
        return [
            vmem(BF16, NX, NY, HALF, channels),
            *[vmem(BF16, NY, HALF, channels) for _ in range(4)],
            vmem(BF16, NY, NZ, ROWS, channels),
            vmem(BF16, NZ - 1, NY, ROWS, channels),
            vmem(BF16, ROWS, channels),
        ]

    scratch = [
        *exact(),
        *exact(),
        vmem(BF16, NX, NY, NZ, ROWS, channels),
        vmem(F32, ROWS, channels),
        vmem(F32, 3, HALF, channels),
        vmem(BF16, NX, NY, HALF, channels),
        *[vmem(BF16, NY, HALF, channels) for _ in range(4)],
        vmem(BF16, NY, NZ, ROWS, channels),
        vmem(F32, NY, NZ, ROWS, channels),
        vmem(BF16, NZ - 1, NY, ROWS, channels),
        vmem(F32, NY, ROWS, channels),
        vmem(F32, ROWS, channels),
        vmem(F32, HALF, channels),
        vmem(F32, HALF, 128),
        vmem(F32, NX, 8, 128),
        vmem(F32, NX - 1, 8, 128),
        vmem(F32, 8, 128),
        vmem(F32, NZ - 1, 8, 128),
        vmem(F32, 8, 128),
        vmem(F32, 8, 128),
        vmem(F32, 8, 128),
        vmem(F32, 3, 8, 128),
        vmem(F32, 3, 8, 128),
        vmem(F32, 7, 8, 128),
        vmem(F32, 7, 8, 128),
        vmem(jnp.int32, queries_dp, 1),
        pltpu.SemaphoreType.DMA((N_SEMS,)),
        pltpu.SemaphoreType.DMA((N_SEMS,)),
    ]
    loss, grad, mean = pl.pallas_call(
        lambda *refs: kernel(count_all, *refs),
        out_shape=(
            jax.ShapeDtypeStruct((1, ROWS), F32),
            jax.ShapeDtypeStruct((ROWS, channels), F32),
            jax.ShapeDtypeStruct((1, 128), F32),
        ),
        in_specs=[pl.BlockSpec(memory_space=pltpu.VMEM)] * 4,
        out_specs=[pl.BlockSpec(memory_space=pltpu.VMEM)] * 3,
        scratch_shapes=scratch,
        compiler_params=pltpu.CompilerParams(
            collective_id=0, has_side_effects=True, vmem_limit_bytes=56 << 20
        ),
        name="patch_nce",
    )(spots, keys, features, bank)
    return (loss.reshape(ROWS), grad, mean[0, 0])


def solution(mesh):
    in_specs = (P("dp", "bank", None), P("dp", None), P("dp"), P("bank", None))
    out_specs = (P(("dp", "bank")), P(("dp", "bank"), None), P())
    return jax.shard_map(
        on_device, mesh=mesh, in_specs=in_specs, out_specs=out_specs, check_vma=False
    )
```

time: 1280 us -> 105 us (0.08)
  the two profiles are of different devices: /device:TPU:16 before, /device:TPU:1 now
where the time goes in v1:
time: 105 us
  Pallas kernels  96.8 us (92%)
  local copies, waits for them, and re-layouts  3.95 us (4%)
  between operations  2.4 us (2%)
  other arithmetic  1.4 us (1%)
    pallas_call x1, Pallas kernels, on_device(): pl.pallas_call(lambda *refs: kernel(count_all, *refs), out_shape=(jax.Sha...  96.8 us
    unnamed x2, local copies, waits for them, and re-layouts  2.51 us

profile of v1, /device:TPU:1, one launch (start us, length us, event | category | flops | bytes accessed | tf_op | source)
XLA Modules:
  0.0 104.6 jit_solution(4901931266567097457)
XLA Ops:
  0.6 0.7 broadcast_subtract_fusion
  1.3 0.7 subtract_bitcast_fusion
  2.0 0.7 copy.13
  2.8 0.7 copy.12
  3.5 96.8 %patch_nce.1 = (f32[1,32]{1,0:T(1,128)}, f32[32,256]{1,0:T(8,128)}, f32[1,128]{1,0:T(1,128)}) custom-call(s32[128,16]{1,0:T(8,128)} %bitcast.8, s32[128,16]{1,0:T(8,128)} %bitcast.7, bf16[16,64,256]{2,1,0:T(8,128)(2,1)} %refs_2_.1, bf16[4096,256]{1,0:T(8,128)(2,1)} %refs_3_.1), custom_call_target="tpu_custom_call" | custom-call | tf_op jit(solution)/shard_map/patch_nce/pallas_call | solution.py:406
  100.3 1.1 %copy.17 = f32[32]{0:T(128)} copy(f32[32]{0:T(128)} %bitcast.10) | data formatting | bytes 256
  101.5 1.4 %copy.18 = f32[32,256]{1,0:T(8,128)} copy(f32[32,256]{1,0:T(8,128)} %get-tuple-element.13) | data formatting | bytes 65536

commit v2 on v0

v2 whole, which is shorter than its diff:
```python
import itertools
import math

import jax
import jax.numpy as jnp
from jax import lax
from jax.experimental import pallas as pl
from jax.experimental.pallas import tpu as pltpu
from jax.sharding import PartitionSpec as P

SOFTMAX_TEMP = 0.07
EPSILON = 1e-05
MESH = pl.DeviceIdType.MESH
F32, BF16 = jnp.float32, jnp.bfloat16

NY, NX, NZ, ND = 2, 4, 8, 4
NG = NY * NZ
ROWS = 32
CHUNKS = 2
PART = ROWS // CHUNKS
HALF = NZ * PART
N_SEMS = 208


def bank_id(y, x, z):
    return (y * NX + x) * NZ + z


def kernel(
    count_all,
    patch_ref,
    pos_ref,
    feat_hbm,
    bank_hbm,
    loss_ref,
    grad_ref,
    mean_ref,
    feat_ref, bank_ref,
    fb, fa, fu, fm, fc, fs, fz,
    pb, pa, pu, pm, pc, ps, pz,
    qa, raw,
    wf, wb, wa, wu, wm, wc, ws, wo, wz,
    acc, tacc,
    ts, tx, tg, ms,
    col,
    ssem, rsem, lsem,
):
    load_feat = pltpu.make_async_copy(feat_hbm, feat_ref, lsem.at[0])
    load_bank = pltpu.make_async_copy(bank_hbm, bank_ref, lsem.at[1])
    load_feat.start()
    load_bank.start()
    place, dp = lax.axis_index("bank"), lax.axis_index("dp")
    y, x, z = place // (NX * NZ), (place // NZ) % NX, place % NZ
    xp, xo, xm = (x + 1) % NX, (x + 2) % NX, (x + 3) % NX
    x_peers = [{"bank": bank_id(y, (x + k) % NX, z)} for k in range(1, NX)]
    plus, minus = x_peers[0], x_peers[2]
    here = y * NZ + z
    g_at = [((here + k) % NG // NZ, (here + k) % NZ) for k in range(1, NG)]
    g_peers = [{"bank": bank_id(gy, x, gz)} for gy, gz in g_at]
    spot = x * ND + dp
    m_peers = []
    for k in range(1, NX * ND):
        other = (spot + k) % (NX * ND)
        m_peers.append({"dp": other % ND, "bank": bank_id(y, other // ND, z)})
    count = itertools.count()

    def remote(src, dst, peer):
        i = next(count)
        return pltpu.make_async_remote_copy(
            src_ref=src,
            dst_ref=dst,
            send_sem=ssem.at[i],
            recv_sem=rsem.at[i],
            device_id=peer,
            device_id_type=MESH,
        )

    started = []

    def go(*copies):
        for copy in copies:
            copy.start()
            started.append(copy)

    def arrived(*copies):
        for copy in copies:
            copy.wait_recv()

    barrier = pltpu.get_barrier_semaphore()
    greeted = g_peers + m_peers
    for peer in greeted:
        pl.semaphore_signal(barrier, inc=1, device_id=peer, device_id_type=MESH)

    images, spots, channels = feat_ref.shape
    patches = patch_ref.shape[1]
    spread = jnp.transpose(patch_ref[...] - place * spots)
    load_feat.wait()
    for i in range(images):
        hit = spread[:, i : i + 1] == lax.broadcasted_iota(jnp.int32, (patches, spots), 1)
        picked = jnp.dot(hit.astype(BF16), feat_ref[i], preferred_element_type=F32).astype(BF16)
        picked = picked.reshape(patches // ROWS, CHUNKS, PART, channels)
        first = i * patches
        at = first // (NZ * ROWS)
        row = first % (NZ * ROWS) // CHUNKS
        for c in range(CHUNKS):
            fb[c, at % NX, at // NX, pl.ds(row, patches // CHUNKS), :] = picked[:, c].reshape(
                patches // CHUNKS, channels
            )
    pl.semaphore_wait(barrier, len(greeted))

    def over_x(b, a, u, m, c):
        return (
            [remote(b.at[xo, 0], a.at[0], plus), remote(b.at[xo, 1], a.at[1], minus)],
            [remote(b.at[xp, 1], u.at[1], plus), remote(b.at[xm, 0], u.at[0], minus)],
            [remote(m.at[0], c.at[0], plus), remote(m.at[1], c.at[1], minus)],
        )

    def merge(b, a, m, copies):
        arrived(copies[0][0])
        m[0] = a[0] + b[xp, 0]
        go(copies[2][0])
        arrived(copies[0][1])
        m[1] = a[1] + b[xm, 1]
        go(copies[2][1])

    def x_total(b, u, c, s, copies):
        arrived(*copies[1], *copies[2])
        for h in range(NY):
            s[h] = (b[x, h] + u[h] + c[h]).reshape(s.shape[1:])

    def over_group(s, r):
        return [
            remote(s.at[gy, gz], r.at[k], peer)
            for k, ((gy, gz), peer) in enumerate(zip(g_at, g_peers))
        ]

    def g_total(s, r, copies):
        total = s[y, z]
        for k, copy in enumerate(copies):
            arrived(copy)
            total = total + r[k]
        return total

    bank_dev = bank_ref.shape[0]
    wide = 2048

    def take(low, high):
        def block(at, carry):
            rows = col[pl.ds(pl.multiple_of(at * NZ * ROWS, NZ * ROWS), NZ * ROWS), :]
            acc[...] = jnp.zeros_like(acc)

            def some(j, _):
                start = pl.multiple_of(j * wide, wide)
                keys = lax.broadcasted_iota(jnp.int32, (NZ * ROWS, wide), 1) + start
                one = jnp.where(rows == keys, 1.0, 0.0).astype(BF16)
                acc[...] = acc[...] + jnp.dot(
                    one, bank_ref[pl.ds(start, wide), :], preferred_element_type=F32
                )
                return 0

            lax.fori_loop(0, bank_dev // wide, some, 0)
            pb[at % NX, at // NX] = acc[...].astype(BF16)
            return carry

        lax.fori_loop(low, high, block, 0)

    f = [over_x(fb.at[c], fa.at[c], fu.at[c], fm.at[c], fc.at[c]) for c in range(CHUNKS)]
    fg = [over_group(fs.at[c], fz.at[c]) for c in range(CHUNKS)]
    go(*f[0][0], *f[0][1], *f[1][0])
    spread = jnp.transpose(pos_ref[...] - place * bank_dev)
    for g in range(pos_ref.shape[0]):
        col[pl.ds(g * 128, 128), :] = spread[:, g : g + 1]
    load_bank.wait()
    take(0, 2)
    merge(fb.at[0], fa.at[0], fm.at[0], f[0])
    go(*f[1][1])
    take(2, 3)
    merge(fb.at[1], fa.at[1], fm.at[1], f[1])
    take(3, 5)
    x_total(fb.at[0], fu.at[0], fc.at[0], fs.at[0], f[0])
    go(*fg[0])
    take(5, 6)
    x_total(fb.at[1], fu.at[1], fc.at[1], fs.at[1], f[1])
    go(*fg[1])
    take(6, 8)
    p = over_x(pb, pa, pu, pm, pc)
    pg = over_group(ps, pz)
    go(*p[0], *p[1])

    def unit_rows(own):
        scale = lax.rsqrt(jnp.mean(own * own, axis=-1, keepdims=True) + EPSILON)
        return own * scale / math.sqrt(channels)

    qg = []
    for c in range(CHUNKS):
        own = g_total(fs.at[c], fz.at[c], fg[c]).astype(F32)
        raw[pl.ds(c * PART, PART), :] = own
        qa[c, x, y, z] = unit_rows(own).astype(BF16)
        mine = qa.at[c, x, y, z]
        qg.append([remote(mine, mine, peer) for peer in g_peers])
        go(*qg[c])
    merge(pb, pa, pm, p)

    def spread_x(c):
        return (
            [remote(qa.at[c, x, 0], qa.at[c, x, 0], plus), remote(qa.at[c, x, 1], qa.at[c, x, 1], minus)],
            [remote(qa.at[c, x, 1], qa.at[c, x, 1], plus), remote(qa.at[c, x, 0], qa.at[c, x, 0], minus)],
            [remote(qa.at[c, xm, 0], qa.at[c, xm, 0], plus), remote(qa.at[c, xp, 1], qa.at[c, xp, 1], minus)],
        )

    qx = [spread_x(c) for c in range(CHUNKS)]
    factor = 1.0 / (SOFTMAX_TEMP * math.log(2.0))
    block_keys = 2048

    def unit(c, at):
        query = qa[c, at].reshape(NY * HALF, channels)
        acc[...] = jnp.zeros_like(acc)
        tacc[...] = jnp.zeros_like(tacc)

        def step(j, _):
            keys = bank_ref[pl.ds(pl.multiple_of(j * block_keys, block_keys), block_keys), :]
            dots = lax.dot_general(
                query, keys, (((1,), (1,)), ((), ())), preferred_element_type=F32
            )
            terms = jnp.exp2(dots * factor - factor)
            some = terms[:, :128]
            for lane in range(128, block_keys, 128):
                some = some + terms[:, lane : lane + 128]
            tacc[...] = tacc[...] + some
            acc[...] = acc[...] + jnp.dot(terms.astype(BF16), keys, preferred_element_type=F32)
            return 0

        lax.fori_loop(0, bank_dev // block_keys, step, 0)
        sums = jnp.sum(jnp.transpose(tacc[...]), axis=0, keepdims=True)
        for h in range(NY):
            ts[at, pl.ds(NY * c + h, 1), :] = sums[:, h * HALF : (h + 1) * HALF]

    ts[...] = jnp.zeros_like(ts)
    arrived(*qg[0])
    go(*qx[0][0], *qx[0][1])
    unit(0, x)
    wo[0] = acc[...].reshape(wo.shape[1:])
    arrived(*qx[0][0])
    go(*qx[0][2])
    arrived(*qg[1])
    go(*qx[1][0], *qx[1][1])
    x_total(pb, pu, pc, ps, p)
    go(*pg)
    arrived(*qx[0][1])
    w = [over_x(wb.at[c], wa.at[c], wu.at[c], wm.at[c], wc.at[c]) for c in range(CHUNKS)]
    wg = [over_group(ws.at[c], wz.at[c]) for c in range(CHUNKS)]

    def push_plus(c):
        unit(c, xp)
        wf[c] = acc[pl.ds(0, HALF), :]
        wb[c, xp, 1] = acc[pl.ds(HALF, HALF), :].astype(BF16)
        go(w[c][1][0])

    def push_across(c):
        unit(c, xo)
        wb[c, xo, 0] = acc[pl.ds(0, HALF), :].astype(BF16)
        wb[c, xo, 1] = acc[pl.ds(HALF, HALF), :].astype(BF16)
        go(*w[c][0])

    def push_minus(c):
        unit(c, xm)
        wb[c, xm, 0] = acc[pl.ds(0, HALF), :].astype(BF16)
        go(w[c][1][1])
        arrived(*w[c][0])
        wm[c, 0] = (wa[c, 0].astype(F32) + wf[c]).astype(BF16)
        go(w[c][2][0])
        wm[c, 1] = (wa[c, 1].astype(F32) + acc[pl.ds(HALF, HALF), :]).astype(BF16)
        go(w[c][2][1])

    def push_total(c):
        arrived(*w[c][1], *w[c][2])
        for h in range(NY):
            part = wu[c, h].astype(F32) + wc[c, h].astype(F32)
            part = wo[c, h] + part.reshape(NZ, PART, channels)
            wo[c, h] = part
            ws[c, h] = part.astype(BF16)
        go(*wg[c])

    push_plus(0)
    arrived(*qx[1][0])
    go(*qx[1][2])
    arrived(*qx[0][2])
    push_across(0)
    push_minus(0)
    arrived(*qx[1][1], *qx[1][2])
    push_across(1)
    push_plus(1)
    positive = g_total(ps, pz, pg).astype(F32)
    query = qa[:, x, y, z].reshape(ROWS, channels).astype(F32)
    matched = jnp.sum(query * positive, axis=1, keepdims=True) / SOFTMAX_TEMP
    push_total(0)
    push_minus(1)
    t1 = [remote(ts.at[(x + k) % NX], tx.at[k - 1], x_peers[k - 1]) for k in range(1, NX)]
    go(*t1)
    unit(1, x)
    wo[1] = acc[...].reshape(wo.shape[1:])

    total = ts[x]
    for k, copy in enumerate(t1):
        arrived(copy)
        total = total + tx[k]
    line = lax.broadcasted_iota(jnp.int32, (8, 128), 0)
    tg[here] = jnp.where(
        line == 4, jnp.broadcast_to(jnp.sum(matched, axis=0, keepdims=True), (8, 128)), total
    )
    t2 = [remote(tg.at[here], tg.at[here], peer) for peer in g_peers]
    go(*t2)
    push_total(1)
    arrived(*t2)
    total = tg[0]
    for k in range(1, NG):
        total = total + tg[k]
    lane = lax.broadcasted_iota(jnp.int32, (PART, HALF), 1)
    row = lax.broadcasted_iota(jnp.int32, (PART, HALF), 0)
    parts = []
    for c in range(CHUNKS):
        sums = jnp.where(y == 0, total[NY * c : NY * c + 1], total[NY * c + 1 : NY * c + 2])
        mine = jnp.where(lane == row + z * PART, jnp.broadcast_to(sums, (PART, HALF)), 0.0)
        parts.append(jnp.sum(mine, axis=1, keepdims=True))
    exponent_sum = jnp.concatenate(parts, axis=0)
    logs = jnp.sum(jnp.log(total[: NY * CHUNKS]), axis=0, keepdims=True)
    logs = jnp.sum(logs, axis=1, keepdims=True)
    quarter = logs + NG * ROWS / SOFTMAX_TEMP - total[4:5, :1]
    ms[spot] = jnp.broadcast_to(quarter, (8, 128))
    m1 = [remote(ms.at[spot], ms.at[spot], peer) for peer in m_peers]
    go(*m1)

    loss = jnp.log(exponent_sum) + 1.0 / SOFTMAX_TEMP - matched
    diagonal = lax.broadcasted_iota(jnp.int32, (ROWS, ROWS), 0) == lax.broadcasted_iota(
        jnp.int32, (ROWS, ROWS), 1
    )
    loss_ref[...] = jnp.sum(
        jnp.where(diagonal, jnp.broadcast_to(loss, (ROWS, ROWS)), 0.0), axis=0, keepdims=True
    )
    own = raw[...]
    scale = lax.rsqrt(jnp.mean(own * own, axis=-1, keepdims=True) + EPSILON)
    for c in range(CHUNKS):
        weighted = wo[c, y, z]
        for k, copy in enumerate(wg[c]):
            arrived(copy)
            weighted = weighted + wz[c, k].astype(F32)
        some = slice(c * PART, (c + 1) * PART)
        step = (weighted / exponent_sum[some] - positive[some]) / SOFTMAX_TEMP
        inner = jnp.mean(step * own[some], axis=-1, keepdims=True)
        s = scale[some]
        grad_ref[pl.ds(c * PART, PART), :] = (s / math.sqrt(channels)) * (
            step - own[some] * (s * s * inner)
        )
    arrived(*m1)
    losses = ms[0]
    for k in range(1, NX * ND):
        losses = losses + ms[k]
    mean_ref[...] = losses[:1] / count_all
    for copy in started:
        copy.wait_send()


def on_device(features, patch_index, positive_index, bank):
    images, hw_dev, channels = features.shape
    queries_dp = images * patch_index.shape[1]
    count_all = queries_dp * lax.axis_size("dp")

    def vmem(dtype, *shape):
        return pltpu.VMEM(shape, dtype)

    def chunked(*lead, rows):
        return [
            vmem(BF16, *lead, NX, NY, NZ * rows, channels),
            *[vmem(BF16, *lead, NY, NZ * rows, channels) for _ in range(4)],
            vmem(BF16, *lead, NY, NZ, rows, channels),
            vmem(BF16, *lead, NG - 1, rows, channels),
        ]

    scratch = [
        vmem(BF16, *features.shape),
        vmem(BF16, *bank.shape),
        *chunked(CHUNKS, rows=PART),
        *chunked(rows=ROWS),
        vmem(BF16, CHUNKS, NX, NY, NZ, PART, channels),
        vmem(F32, ROWS, channels),
        vmem(F32, CHUNKS, HALF, channels),
        *chunked(CHUNKS, rows=PART)[:6],
        vmem(F32, CHUNKS, NY, NZ, PART, channels),
        vmem(BF16, CHUNKS, NG - 1, PART, channels),
        vmem(F32, NY * HALF, channels),
        vmem(F32, NY * HALF, 128),
        vmem(F32, NX, 8, 128),
        vmem(F32, NX - 1, 8, 128),
        vmem(F32, NG, 8, 128),
        vmem(F32, NX * ND, 8, 128),
        vmem(jnp.int32, queries_dp, 1),
        pltpu.SemaphoreType.DMA((N_SEMS,)),
        pltpu.SemaphoreType.DMA((N_SEMS,)),
        pltpu.SemaphoreType.DMA((2,)),
    ]
    near, far = pl.BlockSpec(memory_space=pltpu.VMEM), pl.BlockSpec(memory_space=pl.ANY)
    loss, grad, mean = pl.pallas_call(
        lambda *refs: kernel(count_all, *refs),
        out_shape=(
            jax.ShapeDtypeStruct((1, ROWS), F32),
            jax.ShapeDtypeStruct((ROWS, channels), F32),
            jax.ShapeDtypeStruct((1, 128), F32),
        ),
        in_specs=[near, near, far, far],
        out_specs=[near] * 3,
        scratch_shapes=scratch,
        compiler_params=pltpu.CompilerParams(
            collective_id=0, has_side_effects=True, vmem_limit_bytes=56 << 20
        ),
        name="patch_nce",
    )(patch_index, positive_index.reshape(-1, 128), features, bank)
    return (loss.reshape(ROWS), grad, mean[0, 0])


def solution(mesh):
    in_specs = (P("dp", "bank", None), P("dp", None), P("dp"), P("bank", None))
    out_specs = (P(("dp", "bank")), P(("dp", "bank"), None), P())
    return jax.shard_map(
        on_device, mesh=mesh, in_specs=in_specs, out_specs=out_specs, check_vma=False
    )
```

time: 1280 us -> 81 us (0.06)
  the two profiles are of different devices: /device:TPU:16 before, /device:TPU:1 now
where the time goes in v2:
time: 81 us; the launch traced here: 80.8 us
  Pallas kernels  75.9 us (94%)
  local copies, waits for them, and re-layouts  2.55 us (3%)
  between operations  2.38 us (3%)
    pallas_call x1, Pallas kernels, on_device(): pl.pallas_call(lambda *refs: kernel(count_all, *refs), out_shape=(jax.Sha...  75.9 us
    unnamed x2, local copies, waits for them, and re-layouts  2.55 us

profile of v2, /device:TPU:1, one launch (start us, length us, event | category | flops | bytes accessed | tf_op | source)
XLA Modules:
  0.0 80.8 jit_solution(11985969558299680966)
XLA Ops:
  0.6 75.9 %patch_nce.1 = (f32[1,32]{1,0:T(1,128)}, f32[32,256]{1,0:T(8,128)}, f32[1,128]{1,0:T(1,128)}) custom-call(s32[16,128]{1,0:T(8,128)} %refs_0_.1, s32[16,128]{1,0:T(8,128)} %bitcast.4, bf16[16,64,256]{2,1,0:T(8,128)(2,1)} %refs_2_.1, bf16[4096,256]{1,0:T(8,128)(2,1)} %refs_3_.1), custom_call_target="tpu_custom_call" | custom-call | tf_op jit(solution)/shard_map/patch_nce/pallas_call | solution.py:402
  76.5 1.2 %copy.10 = f32[32]{0:T(128)} copy(f32[32]{0:T(128)} %bitcast.6) | data formatting | bytes 256
  77.7 1.4 %copy.11 = f32[32,256]{1,0:T(8,128)} copy(f32[32,256]{1,0:T(8,128)} %get-tuple-element.13) | data formatting | bytes 65536

commit v3 on v2

v3 whole, which is shorter than its diff:
```python
import itertools
import math

import jax
import jax.numpy as jnp
from jax import lax
from jax.experimental import pallas as pl
from jax.experimental.pallas import tpu as pltpu
from jax.sharding import PartitionSpec as P

SOFTMAX_TEMP = 0.07
EPSILON = 1e-05
MESH = pl.DeviceIdType.MESH
F32, BF16 = jnp.float32, jnp.bfloat16

NY, NX, NZ, ND = 2, 4, 8, 4
NG = NY * NZ
ROWS = 32
CHUNKS = 2
PART = ROWS // CHUNKS
HALF = NZ * PART
N_SEMS = 48


def bank_id(y, x, z):
    return (y * NX + x) * NZ + z


def kernel(
    count_all,
    patch_hbm,
    pos_hbm,
    feat_hbm,
    bank_hbm,
    loss_ref,
    grad_ref,
    mean_ref,
    patch_ref, pos_ref, feat_ref, bank_ref,
    fb, fa, fu, fm, fc, fs, fz,
    pb, pa, pu, pm, pc, ps, pz,
    qa, raw,
    wf, wb, wa, wu, wm, wc, ws, wo, wz,
    acc, tacc,
    ts, tx, tg, ms,
    col,
    sems, lsem,
):
    loads = [
        pltpu.make_async_copy(far, near, lsem.at[i])
        for i, (far, near) in enumerate(
            [(patch_hbm, patch_ref), (feat_hbm, feat_ref), (pos_hbm, pos_ref), (bank_hbm, bank_ref)]
        )
    ]
    for load in loads:
        load.start()
    place, dp = lax.axis_index("bank"), lax.axis_index("dp")
    y, x, z = place // (NX * NZ), (place // NZ) % NX, place % NZ
    xp, xo, xm = (x + 1) % NX, (x + 2) % NX, (x + 3) % NX
    x_peers = [{"bank": bank_id(y, (x + k) % NX, z)} for k in range(1, NX)]
    plus, minus = x_peers[0], x_peers[2]
    here = y * NZ + z
    g_at = [((here + k) % NG // NZ, (here + k) % NZ) for k in range(1, NG)]
    g_peers = [{"bank": bank_id(gy, x, gz)} for gy, gz in g_at]
    spot = x * ND + dp
    m_peers = []
    for k in range(1, NX * ND):
        other = (spot + k) % (NX * ND)
        m_peers.append({"dp": other % ND, "bank": bank_id(y, other // ND, z)})
    count = itertools.count()
    sent = []

    def channel():
        return sems.at[next(count)]

    def remote(src, dst, peer, out, into):
        return pltpu.make_async_remote_copy(
            src_ref=src,
            dst_ref=dst,
            send_sem=out,
            recv_sem=into,
            device_id=peer,
            device_id_type=MESH,
        )

    def take_all(sized, sem):
        pltpu.make_async_copy(sized, sized, sem).wait()

    def go(*copies):
        for copy in copies:
            copy.start()

    barrier = pltpu.get_barrier_semaphore()
    greeted = g_peers + m_peers
    for peer in greeted:
        pl.semaphore_signal(barrier, inc=1, device_id=peer, device_id_type=MESH)

    images, spots, channels = feat_ref.shape
    patches = patch_ref.shape[1]
    loads[0].wait()
    columns = jnp.transpose(patch_ref[...] - place * spots)
    loads[1].wait()
    for i in range(images):
        hit = columns[:, i : i + 1] == lax.broadcasted_iota(jnp.int32, (patches, spots), 1)
        picked = jnp.dot(hit.astype(BF16), feat_ref[i], preferred_element_type=F32).astype(BF16)
        picked = picked.reshape(patches // ROWS, CHUNKS, PART, channels)
        first = i * patches
        at = first // (NZ * ROWS)
        row = first % (NZ * ROWS) // CHUNKS
        for c in range(CHUNKS):
            fb[c, at % NX, at // NX, pl.ds(row, patches // CHUNKS), :] = picked[:, c].reshape(
                patches // CHUNKS, channels
            )
    pl.semaphore_wait(barrier, len(greeted))

    def over_x(b, a, u, m, c):
        out, across, last = channel(), channel(), channel()
        sent.append((b.at[pl.ds(0, 3)], out))
        return (
            [
                remote(b.at[xo, 0], a.at[0], plus, out, across),
                remote(b.at[xo, 1], a.at[1], minus, out, across),
            ],
            [
                remote(b.at[xp, 1], u.at[1], plus, out, last),
                remote(b.at[xm, 0], u.at[0], minus, out, last),
            ],
            [
                remote(m.at[0], c.at[0], plus, out, last),
                remote(m.at[1], c.at[1], minus, out, last),
            ],
            (a, across),
            (b.at[pl.ds(0, 2)], last),
        )

    def merge(b, a, m, copies):
        take_all(*copies[3])
        m[0] = a[0] + b[xp, 0]
        m[1] = a[1] + b[xm, 1]
        go(*copies[2])

    def x_total(b, u, c, s, copies):
        take_all(*copies[4])
        for h in range(NY):
            s[h] = (b[x, h] + u[h] + c[h]).reshape(s.shape[1:])

    def over_group(s, r):
        out, into = channel(), channel()
        sent.append((r, out))
        copies = [
            remote(s.at[gy, gz], r.at[k], peer, out, into)
            for k, ((gy, gz), peer) in enumerate(zip(g_at, g_peers))
        ]
        return copies, (r, into)

    def g_total(s, r, stage):
        take_all(*stage[1])
        total = s[y, z]
        for k in range(NG - 1):
            total = total + r[k]
        return total

    bank_dev = bank_ref.shape[0]
    wide = 2048

    def take(at, h):
        first = pl.multiple_of((h * NX + at) * NZ * ROWS, NZ * ROWS)
        rows = col[pl.ds(first, NZ * ROWS), :]
        acc[...] = jnp.zeros_like(acc)

        def some(j, _):
            start = pl.multiple_of(j * wide, wide)
            keys = lax.broadcasted_iota(jnp.int32, (NZ * ROWS, wide), 1) + start
            one = jnp.where(rows == keys, 1.0, 0.0).astype(BF16)
            acc[...] = acc[...] + jnp.dot(
                one, bank_ref[pl.ds(start, wide), :], preferred_element_type=F32
            )
            return 0

        lax.fori_loop(0, bank_dev // wide, some, 0)
        pb[at, h] = acc[...].astype(BF16)

    f = [over_x(fb.at[c], fa.at[c], fu.at[c], fm.at[c], fc.at[c]) for c in range(CHUNKS)]
    fg = [over_group(fs.at[c], fz.at[c]) for c in range(CHUNKS)]
    go(*f[0][0], *f[0][1], *f[1][0])
    loads[2].wait()
    columns = jnp.transpose(pos_ref[...] - place * bank_dev)
    for g in range(pos_ref.shape[0]):
        col[pl.ds(g * 128, 128), :] = columns[:, g : g + 1]
    loads[3].wait()
    p = over_x(pb, pa, pu, pm, pc)
    pg = over_group(ps, pz)
    take(xo, 0)
    take(xo, 1)
    merge(fb.at[0], fa.at[0], fm.at[0], f[0])
    go(*f[1][1])
    take(xp, 1)
    merge(fb.at[1], fa.at[1], fm.at[1], f[1])
    take(xm, 0)
    x_total(fb.at[0], fu.at[0], fc.at[0], fs.at[0], f[0])
    go(*fg[0][0])
    go(*p[0], *p[1])
    take(xp, 0)
    take(xm, 1)
    x_total(fb.at[1], fu.at[1], fc.at[1], fs.at[1], f[1])
    go(*fg[1][0])
    take(x, 0)
    take(x, 1)
    merge(pb, pa, pm, p)

    def unit_rows(own):
        scale = lax.rsqrt(jnp.mean(own * own, axis=-1, keepdims=True) + EPSILON)
        return own * scale / math.sqrt(channels)

    near_peers = [{"bank": bank_id(y, x, (z + k) % NZ)} for k in range(1, NZ)]
    far_peers = [{"bank": bank_id(1 - y, x, (z + k) % NZ)} for k in range(NZ)]

    def spread(c):
        out, near, far, one, two, relayed = (channel() for _ in range(6))
        sent.append((fz.at[c], out))
        more = channel()
        sent.append((fb.at[c, pl.ds(0, 3)], more))
        own = qa.at[c, x, y, z]
        mine, other = qa.at[c, x, y], qa.at[c, x, 1 - y]

        def forward(h):
            source = qa.at[c, (x + 3 + 2 * h) % NX, h]
            target = {"bank": bank_id(y, (x + 1 + 2 * h) % NX, z)}
            return remote(source, source, target, more, relayed)

        return {
            "z": [remote(own, own, peer, out, near) for peer in near_peers]
            + [remote(own, own, peer, out, far) for peer in far_peers],
            "z_in": (fz.at[c, pl.ds(0, NZ - 1)], near),
            "y_in": (fz.at[c, pl.ds(0, NZ)], far),
            "one": [remote(mine, mine, peer, more, one) for peer in (plus, minus)],
            "one_in": (fb.at[c, 0], one),
            "two": [remote(other, other, peer, more, two) for peer in (plus, minus)],
            "two_in": (fb.at[c, 0], two),
            "first": [forward(y)],
            "second": [forward(1 - y)],
            "relay_in": (fb.at[c, 0], relayed),
        }

    q = [spread(c) for c in range(CHUNKS)]

    def query_rows(c):
        own = g_total(fs.at[c], fz.at[c], fg[c]).astype(F32)
        raw[pl.ds(c * PART, PART), :] = own
        qa[c, x, y, z] = unit_rows(own).astype(BF16)
        go(*q[c]["z"])

    query_rows(0)
    query_rows(1)

    factor = 1.0 / (SOFTMAX_TEMP * math.log(2.0))
    block_keys = 2048

    def unit(c, at):
        query = qa[c, at].reshape(NY * HALF, channels)
        acc[...] = jnp.zeros_like(acc)
        tacc[...] = jnp.zeros_like(tacc)

        def step(j, _):
            keys = bank_ref[pl.ds(pl.multiple_of(j * block_keys, block_keys), block_keys), :]
            dots = lax.dot_general(
                query, keys, (((1,), (1,)), ((), ())), preferred_element_type=F32
            )
            terms = jnp.exp2(dots * factor - factor)
            some = terms[:, :128]
            for lane in range(128, block_keys, 128):
                some = some + terms[:, lane : lane + 128]
            tacc[...] = tacc[...] + some
            acc[...] = acc[...] + jnp.dot(terms.astype(BF16), keys, preferred_element_type=F32)
            return 0

        lax.fori_loop(0, bank_dev // block_keys, step, 0)
        sums = jnp.sum(jnp.transpose(tacc[...]), axis=0, keepdims=True)
        for h in range(NY):
            ts[at, pl.ds(NY * c + h, 1), :] = sums[:, h * HALF : (h + 1) * HALF]

    ts[...] = jnp.zeros_like(ts)
    w = [over_x(wb.at[c], wa.at[c], wu.at[c], wm.at[c], wc.at[c]) for c in range(CHUNKS)]
    wg = [over_group(ws.at[c], wz.at[c]) for c in range(CHUNKS)]

    def push_own(c):
        unit(c, x)
        wo[c] = acc[...].reshape(wo.shape[1:])

    def push_plus(c):
        unit(c, xp)
        wf[c, 0] = acc[pl.ds(0, HALF), :]
        wb[c, xp, 1] = acc[pl.ds(HALF, HALF), :].astype(BF16)

    def push_minus(c):
        unit(c, xm)
        wf[c, 1] = acc[pl.ds(HALF, HALF), :]
        wb[c, xm, 0] = acc[pl.ds(0, HALF), :].astype(BF16)

    def push_across(c):
        unit(c, xo)
        wb[c, xo, 0] = acc[pl.ds(0, HALF), :].astype(BF16)
        wb[c, xo, 1] = acc[pl.ds(HALF, HALF), :].astype(BF16)

    def push_merged(c):
        take_all(*w[c][3])
        for h in range(NY):
            wm[c, h] = (wa[c, h].astype(F32) + wf[c, h]).astype(BF16)
        go(*w[c][2])

    def push_total(c):
        take_all(*w[c][4])
        for h in range(NY):
            part = wu[c, h].astype(F32) + wc[c, h].astype(F32)
            part = wo[c, h] + part.reshape(NZ, PART, channels)
            wo[c, h] = part
            ws[c, h] = part.astype(BF16)
        go(*wg[c][0])

    take_all(*q[0]["z_in"])
    go(*q[0]["one"])
    take_all(*q[0]["y_in"])
    go(*q[0]["two"])
    push_own(0)
    take_all(*q[0]["one_in"])
    go(*q[0]["first"])
    take_all(*q[1]["z_in"])
    go(*q[1]["one"])
    take_all(*q[0]["two_in"])
    go(*q[0]["second"])
    x_total(pb, pu, pc, ps, p)
    go(*pg[0])
    take_all(*q[1]["y_in"])
    go(*q[1]["two"])
    push_own(1)
    push_plus(0)
    take_all(*q[1]["one_in"])
    go(*q[1]["first"])
    go(w[0][1][0])
    take_all(*q[0]["relay_in"])
    push_across(0)
    take_all(*q[1]["two_in"])
    go(*q[1]["second"])
    go(*w[0][0])
    push_minus(0)
    go(w[0][1][1])
    take_all(*q[1]["relay_in"])
    push_across(1)
    go(*w[1][0])
    push_merged(0)
    push_plus(1)
    go(w[1][1][0])
    positive = g_total(ps, pz, pg).astype(F32)
    query = qa[:, x, y, z].reshape(ROWS, channels).astype(F32)
    matched = jnp.sum(query * positive, axis=1, keepdims=True) / SOFTMAX_TEMP
    push_minus(1)
    t1_out, t1_in = channel(), channel()
    sent.append((tx, t1_out))
    go(
        *[
            remote(ts.at[(x + k) % NX], tx.at[k - 1], x_peers[k - 1], t1_out, t1_in)
            for k in range(1, NX)
        ]
    )
    push_merged(1)
    go(w[1][1][1])

    take_all(tx, t1_in)
    total = ts[x]
    for k in range(NX - 1):
        total = total + tx[k]
    line = lax.broadcasted_iota(jnp.int32, (8, 128), 0)
    tg[here] = jnp.where(
        line == 4, jnp.broadcast_to(jnp.sum(matched, axis=0, keepdims=True), (8, 128)), total
    )
    t2_out, t2_in = channel(), channel()
    others = tg.at[pl.ds(0, NG - 1)]
    sent.append((others, t2_out))
    go(*[remote(tg.at[here], tg.at[here], peer, t2_out, t2_in) for peer in g_peers])
    push_total(0)
    push_total(1)
    take_all(others, t2_in)
    total = tg[0]
    for k in range(1, NG):
        total = total + tg[k]
    lane = lax.broadcasted_iota(jnp.int32, (PART, HALF), 1)
    row = lax.broadcasted_iota(jnp.int32, (PART, HALF), 0)
    parts = []
    for c in range(CHUNKS):
        sums = jnp.where(y == 0, total[NY * c : NY * c + 1], total[NY * c + 1 : NY * c + 2])
        mine = jnp.where(lane == row + z * PART, jnp.broadcast_to(sums, (PART, HALF)), 0.0)
        parts.append(jnp.sum(mine, axis=1, keepdims=True))
    exponent_sum = jnp.concatenate(parts, axis=0)
    logs = jnp.sum(jnp.log(total[: NY * CHUNKS]), axis=0, keepdims=True)
    logs = jnp.sum(logs, axis=1, keepdims=True)
    quarter = logs + NG * ROWS / SOFTMAX_TEMP - total[4:5, :1]
    ms[spot] = jnp.broadcast_to(quarter, (8, 128))
    m1_out, m1_in = channel(), channel()
    rest = ms.at[pl.ds(0, NX * ND - 1)]
    sent.append((rest, m1_out))
    go(*[remote(ms.at[spot], ms.at[spot], peer, m1_out, m1_in) for peer in m_peers])

    loss = jnp.log(exponent_sum) + 1.0 / SOFTMAX_TEMP - matched
    diagonal = lax.broadcasted_iota(jnp.int32, (ROWS, ROWS), 0) == lax.broadcasted_iota(
        jnp.int32, (ROWS, ROWS), 1
    )
    loss_ref[...] = jnp.sum(
        jnp.where(diagonal, jnp.broadcast_to(loss, (ROWS, ROWS)), 0.0), axis=0, keepdims=True
    )
    own = raw[...]
    scale = lax.rsqrt(jnp.mean(own * own, axis=-1, keepdims=True) + EPSILON)
    for c in range(CHUNKS):
        take_all(*wg[c][1])
        weighted = wo[c, y, z]
        for k in range(NG - 1):
            weighted = weighted + wz[c, k].astype(F32)
        some = slice(c * PART, (c + 1) * PART)
        step = (weighted / exponent_sum[some] - positive[some]) / SOFTMAX_TEMP
        inner = jnp.mean(step * own[some], axis=-1, keepdims=True)
        s = scale[some]
        grad_ref[pl.ds(c * PART, PART), :] = (s / math.sqrt(channels)) * (
            step - own[some] * (s * s * inner)
        )
    take_all(rest, m1_in)
    losses = ms[0]
    for k in range(1, NX * ND):
        losses = losses + ms[k]
    mean_ref[...] = losses[:1] / count_all
    for sized, sem in sent:
        take_all(sized, sem)


def on_device(features, patch_index, positive_index, bank):
    images, hw_dev, channels = features.shape
    queries_dp = images * patch_index.shape[1]
    count_all = queries_dp * lax.axis_size("dp")
    positions = positive_index.reshape(-1, 128)

    def vmem(dtype, *shape):
        return pltpu.VMEM(shape, dtype)

    def chunked(*lead, rows):
        return [
            vmem(BF16, *lead, NX, NY, NZ * rows, channels),
            *[vmem(BF16, *lead, NY, NZ * rows, channels) for _ in range(4)],
            vmem(BF16, *lead, NY, NZ, rows, channels),
            vmem(BF16, *lead, NG - 1, rows, channels),
        ]

    scratch = [
        vmem(jnp.int32, *patch_index.shape),
        vmem(jnp.int32, *positions.shape),
        vmem(BF16, *features.shape),
        vmem(BF16, *bank.shape),
        *chunked(CHUNKS, rows=PART),
        *chunked(rows=ROWS),
        vmem(BF16, CHUNKS, NX, NY, NZ, PART, channels),
        vmem(F32, ROWS, channels),
        vmem(F32, CHUNKS, NY, HALF, channels),
        *chunked(CHUNKS, rows=PART)[:6],
        vmem(F32, CHUNKS, NY, NZ, PART, channels),
        vmem(BF16, CHUNKS, NG - 1, PART, channels),
        vmem(F32, NY * HALF, channels),
        vmem(F32, NY * HALF, 128),
        vmem(F32, NX, 8, 128),
        vmem(F32, NX - 1, 8, 128),
        vmem(F32, NG, 8, 128),
        vmem(F32, NX * ND, 8, 128),
        vmem(jnp.int32, queries_dp, 1),
        pltpu.SemaphoreType.DMA((N_SEMS,)),
        pltpu.SemaphoreType.DMA((4,)),
    ]
    near, far = pl.BlockSpec(memory_space=pltpu.VMEM), pl.BlockSpec(memory_space=pl.ANY)
    loss, grad, mean = pl.pallas_call(
        lambda *refs: kernel(count_all, *refs),
        out_shape=(
            jax.ShapeDtypeStruct((1, ROWS), F32),
            jax.ShapeDtypeStruct((ROWS, channels), F32),
            jax.ShapeDtypeStruct((1, 128), F32),
        ),
        in_specs=[far] * 4,
        out_specs=[near] * 3,
        scratch_shapes=scratch,
        compiler_params=pltpu.CompilerParams(
            collective_id=0, has_side_effects=True, vmem_limit_bytes=56 << 20
        ),
        name="patch_nce",
    )(patch_index, positions, features, bank)
    return (loss.reshape(ROWS), grad, mean[0, 0])


def solution(mesh):
    in_specs = (P("dp", "bank", None), P("dp", None), P("dp"), P("bank", None))
    out_specs = (P(("dp", "bank")), P(("dp", "bank"), None), P())
    return jax.shard_map(
        on_device, mesh=mesh, in_specs=in_specs, out_specs=out_specs, check_vma=False
    )
```

time: 81 us -> 73.9 us (0.912)
  Pallas kernels: 75.9 us -> 68.8 us
    pallas_call x1, Pallas kernels: 75.9 us -> 68.8 us  [on_device(): pl.pallas_call(lambda *refs: kernel(count_all, *refs), out_shape=(jax.Sha...]
where the time goes in v3:
time: 73.9 us; the launch traced here: 73.7 us
  Pallas kernels  68.8 us (93%)
  local copies, waits for them, and re-layouts  2.55 us (3%)
  between operations  2.38 us (3%)
    pallas_call x1, Pallas kernels, on_device(): pl.pallas_call(lambda *refs: kernel(count_all, *refs), out_shape=(jax.Sha...  68.8 us
    unnamed x2, local copies, waits for them, and re-layouts  2.55 us

profile of v3, /device:TPU:1, one launch (start us, length us, event | category | flops | bytes accessed | tf_op | source)
XLA Modules:
  0.0 73.7 jit_solution(12409956093469375628)
XLA Ops:
  0.6 68.8 %patch_nce.1 = (f32[1,32]{1,0:T(1,128)}, f32[32,256]{1,0:T(8,128)}, f32[1,128]{1,0:T(1,128)}) custom-call(s32[16,128]{1,0:T(8,128)} %refs_0_.1, s32[16,128]{1,0:T(8,128)} %bitcast.4, bf16[16,64,256]{2,1,0:T(8,128)(2,1)} %refs_2_.1, bf16[4096,256]{1,0:T(8,128)(2,1)} %refs_3_.1), custom_call_target="tpu_custom_call" | custom-call | tf_op jit(solution)/shard_map/patch_nce/pallas_call | solution.py:473
  69.4 1.2 %copy.10 = f32[32]{0:T(128)} copy(f32[32]{0:T(128)} %bitcast.6) | data formatting | bytes 256
  70.6 1.4 %copy.11 = f32[32,256]{1,0:T(8,128)} copy(f32[32,256]{1,0:T(8,128)} %get-tuple-element.13) | data formatting | bytes 65536

commit v4 on v3

--- a/solution.py
+++ b/solution.py
@@ -40,7 +40,7 @@
     pb, pa, pu, pm, pc, ps, pz,
     qa, raw,
     wf, wb, wa, wu, wm, wc, ws, wo, wz,
-    acc, tacc,
+    acc, tacc, held,
     ts, tx, tg, ms,
     col,
     sems, lsem,
@@ -181,7 +181,7 @@
 
     f = [over_x(fb.at[c], fa.at[c], fu.at[c], fm.at[c], fc.at[c]) for c in range(CHUNKS)]
     fg = [over_group(fs.at[c], fz.at[c]) for c in range(CHUNKS)]
-    go(*f[0][0], *f[0][1], *f[1][0])
+    go(*f[0][0], *f[1][0], *f[0][1])
     loads[2].wait()
     columns = jnp.transpose(pos_ref[...] - place * bank_dev)
     for g in range(pos_ref.shape[0]):
@@ -192,20 +192,19 @@
     take(xo, 0)
     take(xo, 1)
     merge(fb.at[0], fa.at[0], fm.at[0], f[0])
-    go(*f[1][1])
     take(xp, 1)
     merge(fb.at[1], fa.at[1], fm.at[1], f[1])
+    go(*f[1][1])
     take(xm, 0)
     x_total(fb.at[0], fu.at[0], fc.at[0], fs.at[0], f[0])
     go(*fg[0][0])
-    go(*p[0], *p[1])
     take(xp, 0)
     take(xm, 1)
     x_total(fb.at[1], fu.at[1], fc.at[1], fs.at[1], f[1])
     go(*fg[1][0])
+    go(*p[0], *p[1])
     take(x, 0)
     take(x, 1)
-    merge(pb, pa, pm, p)
 
     def unit_rows(own):
         scale = lax.rsqrt(jnp.mean(own * own, axis=-1, keepdims=True) + EPSILON)
@@ -250,49 +249,51 @@
         go(*q[c]["z"])
 
     query_rows(0)
+    merge(pb, pa, pm, p)
     query_rows(1)
 
     factor = 1.0 / (SOFTMAX_TEMP * math.log(2.0))
-    block_keys = 2048
-
-    def unit(c, at):
+    block_keys = bank_dev // 2
+
+    def half(c, at, j):
         query = qa[c, at].reshape(NY * HALF, channels)
-        acc[...] = jnp.zeros_like(acc)
-        tacc[...] = jnp.zeros_like(tacc)
-
-        def step(j, _):
-            keys = bank_ref[pl.ds(pl.multiple_of(j * block_keys, block_keys), block_keys), :]
-            dots = lax.dot_general(
-                query, keys, (((1,), (1,)), ((), ())), preferred_element_type=F32
-            )
-            terms = jnp.exp2(dots * factor - factor)
-            some = terms[:, :128]
-            for lane in range(128, block_keys, 128):
-                some = some + terms[:, lane : lane + 128]
+        keys = bank_ref[pl.ds(j * block_keys, block_keys), :]
+        dots = lax.dot_general(query, keys, (((1,), (1,)), ((), ())), preferred_element_type=F32)
+        terms = jnp.exp2(dots * factor - factor)
+        some = terms[:, :128]
+        for lane in range(128, block_keys, 128):
+            some = some + terms[:, lane : lane + 128]
+        pushed = jnp.dot(terms.astype(BF16), keys, preferred_element_type=F32)
+        if j == 0:
+            tacc[...] = some
+            acc[...] = pushed
+        else:
             tacc[...] = tacc[...] + some
-            acc[...] = acc[...] + jnp.dot(terms.astype(BF16), keys, preferred_element_type=F32)
-            return 0
-
-        lax.fori_loop(0, bank_dev // block_keys, step, 0)
+            acc[...] = acc[...] + pushed
+
+    def finish(c, at):
         sums = jnp.sum(jnp.transpose(tacc[...]), axis=0, keepdims=True)
         for h in range(NY):
             ts[at, pl.ds(NY * c + h, 1), :] = sums[:, h * HALF : (h + 1) * HALF]
 
+    def unit(c, at, between=lambda: None):
+        half(c, at, 0)
+        between()
+        half(c, at, 1)
+        finish(c, at)
+
     ts[...] = jnp.zeros_like(ts)
     w = [over_x(wb.at[c], wa.at[c], wu.at[c], wm.at[c], wc.at[c]) for c in range(CHUNKS)]
     wg = [over_group(ws.at[c], wz.at[c]) for c in range(CHUNKS)]
 
-    def push_own(c):
-        unit(c, x)
-        wo[c] = acc[...].reshape(wo.shape[1:])
-
-    def push_plus(c):
-        unit(c, xp)
+    def push_plus(c, between=lambda: None):
+        unit(c, xp, between)
         wf[c, 0] = acc[pl.ds(0, HALF), :]
         wb[c, xp, 1] = acc[pl.ds(HALF, HALF), :].astype(BF16)
-
-    def push_minus(c):
-        unit(c, xm)
+        go(w[c][1][0])
+
+    def push_minus(c, between=lambda: None):
+        unit(c, xm, between)
         wf[c, 1] = acc[pl.ds(HALF, HALF), :]
         wb[c, xm, 0] = acc[pl.ds(0, HALF), :].astype(BF16)
 
@@ -300,6 +301,7 @@
         unit(c, xo)
         wb[c, xo, 0] = acc[pl.ds(0, HALF), :].astype(BF16)
         wb[c, xo, 1] = acc[pl.ds(HALF, HALF), :].astype(BF16)
+        go(*w[c][0])
 
     def push_merged(c):
         take_all(*w[c][3])
@@ -320,35 +322,38 @@
     go(*q[0]["one"])
     take_all(*q[0]["y_in"])
     go(*q[0]["two"])
-    push_own(0)
+    unit(0, x)
+    wo[0] = acc[...].reshape(wo.shape[1:])
     take_all(*q[0]["one_in"])
     go(*q[0]["first"])
     take_all(*q[1]["z_in"])
     go(*q[1]["one"])
+    take_all(*q[1]["y_in"])
+    go(*q[1]["two"])
+    half(1, x, 0)
+    wo[1] = acc[...].reshape(wo.shape[1:])
+    held[...] = tacc[...]
     take_all(*q[0]["two_in"])
     go(*q[0]["second"])
     x_total(pb, pu, pc, ps, p)
     go(*pg[0])
-    take_all(*q[1]["y_in"])
-    go(*q[1]["two"])
-    push_own(1)
-    push_plus(0)
-    take_all(*q[1]["one_in"])
-    go(*q[1]["first"])
-    go(w[0][1][0])
+
+    def relay_first():
+        take_all(*q[1]["one_in"])
+        go(*q[1]["first"])
+
+    def relay_second():
+        take_all(*q[1]["two_in"])
+        go(*q[1]["second"])
+
+    push_plus(0, relay_first)
+    push_minus(0, relay_second)
+    go(w[0][1][1])
     take_all(*q[0]["relay_in"])
     push_across(0)
-    take_all(*q[1]["two_in"])
-    go(*q[1]["second"])
-    go(*w[0][0])
-    push_minus(0)
-    go(w[0][1][1])
     take_all(*q[1]["relay_in"])
     push_across(1)
-    go(*w[1][0])
-    push_merged(0)
-    push_plus(1)
-    go(w[1][1][0])
+    push_plus(1, lambda: push_merged(0))
     positive = g_total(ps, pz, pg).astype(F32)
     query = qa[:, x, y, z].reshape(ROWS, channels).astype(F32)
     matched = jnp.sum(query * positive, axis=1, keepdims=True) / SOFTMAX_TEMP
@@ -363,6 +368,11 @@
     )
     push_merged(1)
     go(w[1][1][1])
+    acc[...] = wo[1].reshape(acc.shape)
+    tacc[...] = held[...]
+    half(1, x, 1)
+    finish(1, x)
+    wo[1] = acc[...].reshape(wo.shape[1:])
 
     take_all(tx, t1_in)
     total = ts[x]
@@ -461,6 +471,7 @@
         vmem(BF16, CHUNKS, NG - 1, PART, channels),
         vmem(F32, NY * HALF, channels),
         vmem(F32, NY * HALF, 128),
+        vmem(F32, NY * HALF, 128),
         vmem(F32, NX, 8, 128),
         vmem(F32, NX - 1, 8, 128),
         vmem(F32, NG, 8, 128),
@@ -473,9 +484,9 @@
     loss, grad, mean = pl.pallas_call(
         lambda *refs: kernel(count_all, *refs),
         out_shape=(
-            jax.ShapeDtypeStruct((1, ROWS), F32),
-            jax.ShapeDtypeStruct((ROWS, channels), F32),
-            jax.ShapeDtypeStruct((1, 128), F32),
+            pltpu.VMEM((1, ROWS), F32),
+            pltpu.VMEM((ROWS, channels), F32),
+            pltpu.VMEM((1, 128), F32),
         ),
         in_specs=[far] * 4,
         out_specs=[near] * 3,

time: 73.9 us -> 69.8 us (0.945)
  Pallas kernels: 68.8 us -> 66.7 us
  local copies, waits for them, and re-layouts: 2.55 us -> 1.13 us
    pallas_call x1, Pallas kernels: 68.8 us -> 66.7 us  [on_device(): pl.pallas_call(lambda *refs: kernel(count_all, *refs), out_shape=(pltpu.V...]
    unnamed x2, local copies, waits for them, and re-layouts: 2.55 us -> 1.13 us
where the time goes in v4:
time: 69.8 us; the launch traced here: 69.6 us
  Pallas kernels  66.7 us (96%)
  between operations  1.81 us (3%)
  local copies, waits for them, and re-layouts  1.13 us (2%)
    pallas_call x1, Pallas kernels, on_device(): pl.pallas_call(lambda *refs: kernel(count_all, *refs), out_shape=(pltpu.V...  66.7 us

profile of v4, /device:TPU:1, one launch (start us, length us, event | category | flops | bytes accessed | tf_op | source)
XLA Modules:
  0.0 69.6 jit_solution(7622398168594313807)
XLA Ops:
  0.6 66.7 %patch_nce.1 = (f32[1,32]{1,0:T(1,128)S(1)}, f32[32,256]{1,0:T(8,128)S(1)}, f32[1,128]{1,0:T(1,128)S(1)}) custom-call(s32[16,128]{1,0:T(8,128)} %refs_0_.1, s32[16,128]{1,0:T(8,128)} %bitcast.6, bf16[16,64,256]{2,1,0:T(8,128)(2,1)} %refs_2_.1, bf16[4096,256]{1,0:T(8,128)(2,1)} %refs_3_.1), custom_call_target="tpu_custom_call" | custom-call | tf_op jit(solution)/shard_map/patch_nce/pallas_call | solution.py:484
  67.3 0.5 copy.10
  67.9 0.6 copy.11

commit v5 on v4

--- a/solution.py
+++ b/solution.py
@@ -43,7 +43,7 @@
     acc, tacc, held,
     ts, tx, tg, ms,
     col,
-    sems, lsem,
+    sems, lsem, heard,
 ):
     loads = [
         pltpu.make_async_copy(far, near, lsem.at[i])
@@ -90,9 +90,20 @@
             copy.start()
 
     barrier = pltpu.get_barrier_semaphore()
-    greeted = g_peers + m_peers
+    z_next = [{"bank": bank_id(y, x, (z + k) % NZ)} for k in (1, NZ - 1)]
+    x_next = [plus, minus]
+    greeted = x_next + z_next + [{"bank": bank_id(1 - y, x, z)}]
+    greeted += [{"dp": (dp + k) % ND, "bank": place} for k in range(1, ND)]
     for peer in greeted:
         pl.semaphore_signal(barrier, inc=1, device_id=peer, device_id_type=MESH)
+
+    def tell(i, peers):
+        for peer in peers:
+            pl.semaphore_signal(heard.at[i], inc=1, device_id=peer, device_id_type=MESH)
+
+    def hear(i):
+        pl.semaphore_wait(heard.at[i], 2)
+
 
     images, spots, channels = feat_ref.shape
     patches = patch_ref.shape[1]
@@ -182,6 +193,8 @@
     f = [over_x(fb.at[c], fa.at[c], fu.at[c], fm.at[c], fc.at[c]) for c in range(CHUNKS)]
     fg = [over_group(fs.at[c], fz.at[c]) for c in range(CHUNKS)]
     go(*f[0][0], *f[1][0], *f[0][1])
+    tell(0, z_next)
+    tell(4, x_next)
     loads[2].wait()
     columns = jnp.transpose(pos_ref[...] - place * bank_dev)
     for g in range(pos_ref.shape[0]):
@@ -190,12 +203,22 @@
     p = over_x(pb, pa, pu, pm, pc)
     pg = over_group(ps, pz)
     take(xo, 0)
+    hear(0)
+    tell(1, z_next)
+    hear(4)
+    tell(5, x_next)
     take(xo, 1)
+    hear(1)
+    tell(2, z_next)
     merge(fb.at[0], fa.at[0], fm.at[0], f[0])
     take(xp, 1)
+    hear(2)
+    tell(3, z_next)
     merge(fb.at[1], fa.at[1], fm.at[1], f[1])
     go(*f[1][1])
     take(xm, 0)
+    hear(3)
+    hear(5)
     x_total(fb.at[0], fu.at[0], fc.at[0], fs.at[0], f[0])
     go(*fg[0][0])
     take(xp, 0)
@@ -297,8 +320,7 @@
         wf[c, 1] = acc[pl.ds(HALF, HALF), :]
         wb[c, xm, 0] = acc[pl.ds(0, HALF), :].astype(BF16)
 
-    def push_across(c):
-        unit(c, xo)
+    def push_halves(c):
         wb[c, xo, 0] = acc[pl.ds(0, HALF), :].astype(BF16)
         wb[c, xo, 1] = acc[pl.ds(HALF, HALF), :].astype(BF16)
         go(*w[c][0])
@@ -324,8 +346,6 @@
     go(*q[0]["two"])
     unit(0, x)
     wo[0] = acc[...].reshape(wo.shape[1:])
-    take_all(*q[0]["one_in"])
-    go(*q[0]["first"])
     take_all(*q[1]["z_in"])
     go(*q[1]["one"])
     take_all(*q[1]["y_in"])
@@ -333,46 +353,45 @@
     half(1, x, 0)
     wo[1] = acc[...].reshape(wo.shape[1:])
     held[...] = tacc[...]
+    take_all(*q[0]["one_in"])
+    go(*q[0]["first"])
     take_all(*q[0]["two_in"])
     go(*q[0]["second"])
     x_total(pb, pu, pc, ps, p)
     go(*pg[0])
-
-    def relay_first():
-        take_all(*q[1]["one_in"])
-        go(*q[1]["first"])
-
-    def relay_second():
-        take_all(*q[1]["two_in"])
-        go(*q[1]["second"])
-
-    push_plus(0, relay_first)
-    push_minus(0, relay_second)
+    push_plus(0)
+    push_minus(0)
+    take_all(*q[1]["one_in"])
+    go(*q[1]["first"])
     go(w[0][1][1])
+    take_all(*q[1]["two_in"])
+    go(*q[1]["second"])
+    push_plus(1)
     take_all(*q[0]["relay_in"])
-    push_across(0)
+    unit(0, xo)
+    push_halves(0)
     take_all(*q[1]["relay_in"])
-    push_across(1)
-    push_plus(1, lambda: push_merged(0))
+    t1_out, t1_in = channel(), channel()
+    sent.append((tx, t1_out))
+    t1 = [
+        remote(ts.at[(x + k) % NX], tx.at[k - 1], x_peers[k - 1], t1_out, t1_in)
+        for k in range(1, NX)
+    ]
+    unit(1, xo)
+    go(t1[1], t1[0])
+    push_halves(1)
     positive = g_total(ps, pz, pg).astype(F32)
     query = qa[:, x, y, z].reshape(ROWS, channels).astype(F32)
     matched = jnp.sum(query * positive, axis=1, keepdims=True) / SOFTMAX_TEMP
-    push_minus(1)
-    t1_out, t1_in = channel(), channel()
-    sent.append((tx, t1_out))
-    go(
-        *[
-            remote(ts.at[(x + k) % NX], tx.at[k - 1], x_peers[k - 1], t1_out, t1_in)
-            for k in range(1, NX)
-        ]
-    )
-    push_merged(1)
+    push_minus(1, lambda: push_merged(0))
+    go(t1[2])
     go(w[1][1][1])
     acc[...] = wo[1].reshape(acc.shape)
     tacc[...] = held[...]
     half(1, x, 1)
     finish(1, x)
     wo[1] = acc[...].reshape(wo.shape[1:])
+    push_merged(1)
 
     take_all(tx, t1_in)
     total = ts[x]
@@ -479,6 +498,7 @@
         vmem(jnp.int32, queries_dp, 1),
         pltpu.SemaphoreType.DMA((N_SEMS,)),
         pltpu.SemaphoreType.DMA((4,)),
+        pltpu.SemaphoreType.REGULAR((6,)),
     ]
     near, far = pl.BlockSpec(memory_space=pltpu.VMEM), pl.BlockSpec(memory_space=pl.ANY)
     loss, grad, mean = pl.pallas_call(

time: 69.8 us -> 66.2 us (0.948)
  Pallas kernels: 66.7 us -> 63.1 us
    pallas_call x1, Pallas kernels: 66.7 us -> 63.1 us  [on_device(): pl.pallas_call(lambda *refs: kernel(count_all, *refs), out_shape=(pltpu.V...]
where the time goes in v5:
time: 66.2 us; the launch traced here: 66 us
  Pallas kernels  63.1 us (95%)
  between operations  1.81 us (3%)
  local copies, waits for them, and re-layouts  1.13 us (2%)
    pallas_call x1, Pallas kernels, on_device(): pl.pallas_call(lambda *refs: kernel(count_all, *refs), out_shape=(pltpu.V...  63.1 us

profile of v5, /device:TPU:1, one launch (start us, length us, event | category | flops | bytes accessed | tf_op | source)
XLA Modules:
  0.0 66.0 jit_solution(18081261474293029970)
XLA Ops:
  0.6 63.1 %patch_nce.1 = (f32[1,32]{1,0:T(1,128)S(1)}, f32[32,256]{1,0:T(8,128)S(1)}, f32[1,128]{1,0:T(1,128)S(1)}) custom-call(s32[16,128]{1,0:T(8,128)} %refs_0_.1, s32[16,128]{1,0:T(8,128)} %bitcast.6, bf16[16,64,256]{2,1,0:T(8,128)(2,1)} %refs_2_.1, bf16[4096,256]{1,0:T(8,128)(2,1)} %refs_3_.1), custom_call_target="tpu_custom_call" | custom-call | tf_op jit(solution)/shard_map/patch_nce/pallas_call | solution.py:504
  63.8 0.5 copy.10
  64.3 0.6 copy.11

commit v6 on v5

--- a/solution.py
+++ b/solution.py
@@ -383,15 +383,15 @@
     positive = g_total(ps, pz, pg).astype(F32)
     query = qa[:, x, y, z].reshape(ROWS, channels).astype(F32)
     matched = jnp.sum(query * positive, axis=1, keepdims=True) / SOFTMAX_TEMP
-    push_minus(1, lambda: push_merged(0))
+    push_minus(1)
     go(t1[2])
+    push_merged(0)
     go(w[1][1][1])
     acc[...] = wo[1].reshape(acc.shape)
     tacc[...] = held[...]
     half(1, x, 1)
     finish(1, x)
     wo[1] = acc[...].reshape(wo.shape[1:])
-    push_merged(1)
 
     take_all(tx, t1_in)
     total = ts[x]
@@ -405,6 +405,7 @@
     others = tg.at[pl.ds(0, NG - 1)]
     sent.append((others, t2_out))
     go(*[remote(tg.at[here], tg.at[here], peer, t2_out, t2_in) for peer in g_peers])
+    push_merged(1)
     push_total(0)
     push_total(1)
     take_all(others, t2_in)

time: 66.2 us -> 65 us (0.982)
  Pallas kernels: 63.1 us -> 61.9 us
    pallas_call x1, Pallas kernels: 63.1 us -> 61.9 us  [on_device(): pl.pallas_call(lambda *refs: kernel(count_all, *refs), out_shape=(pltpu.V...]
where the time goes in v6:
time: 65 us; the launch traced here: 64.9 us
  Pallas kernels  61.9 us (95%)
  between operations  1.81 us (3%)
  local copies, waits for them, and re-layouts  1.13 us (2%)
    pallas_call x1, Pallas kernels, on_device(): pl.pallas_call(lambda *refs: kernel(count_all, *refs), out_shape=(pltpu.V...  61.9 us

profile of v6, /device:TPU:1, one launch (start us, length us, event | category | flops | bytes accessed | tf_op | source)
XLA Modules:
  0.0 64.9 jit_solution(7438908806724727818)
XLA Ops:
  0.6 61.9 %patch_nce.1 = (f32[1,32]{1,0:T(1,128)S(1)}, f32[32,256]{1,0:T(8,128)S(1)}, f32[1,128]{1,0:T(1,128)S(1)}) custom-call(s32[16,128]{1,0:T(8,128)} %refs_0_.1, s32[16,128]{1,0:T(8,128)} %bitcast.6, bf16[16,64,256]{2,1,0:T(8,128)(2,1)} %refs_2_.1, bf16[4096,256]{1,0:T(8,128)(2,1)} %refs_3_.1), custom_call_target="tpu_custom_call" | custom-call | tf_op jit(solution)/shard_map/patch_nce/pallas_call | solution.py:505
  62.6 0.5 copy.10
  63.1 0.6 copy.11

commit v7 on v6

--- a/solution.py
+++ b/solution.py
@@ -278,8 +278,7 @@
     factor = 1.0 / (SOFTMAX_TEMP * math.log(2.0))
     block_keys = bank_dev // 2
 
-    def half(c, at, j):
-        query = qa[c, at].reshape(NY * HALF, channels)
+    def half(query, j):
         keys = bank_ref[pl.ds(j * block_keys, block_keys), :]
         dots = lax.dot_general(query, keys, (((1,), (1,)), ((), ())), preferred_element_type=F32)
         terms = jnp.exp2(dots * factor - factor)
@@ -294,30 +293,44 @@
             tacc[...] = tacc[...] + some
             acc[...] = acc[...] + pushed
 
-    def finish(c, at):
+    def finish(c, places):
         sums = jnp.sum(jnp.transpose(tacc[...]), axis=0, keepdims=True)
-        for h in range(NY):
-            ts[at, pl.ds(NY * c + h, 1), :] = sums[:, h * HALF : (h + 1) * HALF]
-
-    def unit(c, at, between=lambda: None):
-        half(c, at, 0)
-        between()
-        half(c, at, 1)
-        finish(c, at)
+        for i, (at, h) in enumerate(places):
+            ts[at, pl.ds(NY * c + h, 1), :] = sums[:, i * HALF : (i + 1) * HALF]
+
+    def whole(c, at):
+        return qa[c, at].reshape(NY * HALF, channels)
+
+    def unit(c, at):
+        half(whole(c, at), 0)
+        half(whole(c, at), 1)
+        finish(c, [(at, h) for h in range(NY)])
+
+    def pair(c, h):
+        def query():
+            return jnp.concatenate(
+                [qa[c, at, h].reshape(HALF, channels) for at in (xp, xm)], axis=0
+            )
+
+        half(query(), 0)
+        half(query(), 1)
+        finish(c, [(xp, h), (xm, h)])
+        wf[c, 0, h] = acc[pl.ds(0, HALF), :]
+        wf[c, 1, h] = acc[pl.ds(HALF, HALF), :]
 
     ts[...] = jnp.zeros_like(ts)
     w = [over_x(wb.at[c], wa.at[c], wu.at[c], wm.at[c], wc.at[c]) for c in range(CHUNKS)]
     wg = [over_group(ws.at[c], wz.at[c]) for c in range(CHUNKS)]
 
-    def push_plus(c, between=lambda: None):
-        unit(c, xp, between)
-        wf[c, 0] = acc[pl.ds(0, HALF), :]
+    def push_plus(c):
+        unit(c, xp)
+        wf[c, 0, 0] = acc[pl.ds(0, HALF), :]
         wb[c, xp, 1] = acc[pl.ds(HALF, HALF), :].astype(BF16)
         go(w[c][1][0])
 
-    def push_minus(c, between=lambda: None):
-        unit(c, xm, between)
-        wf[c, 1] = acc[pl.ds(HALF, HALF), :]
+    def push_minus(c):
+        unit(c, xm)
+        wf[c, 1, 1] = acc[pl.ds(HALF, HALF), :]
         wb[c, xm, 0] = acc[pl.ds(0, HALF), :].astype(BF16)
 
     def push_halves(c):
@@ -328,7 +341,7 @@
     def push_merged(c):
         take_all(*w[c][3])
         for h in range(NY):
-            wm[c, h] = (wa[c, h].astype(F32) + wf[c, h]).astype(BF16)
+            wm[c, h] = (wa[c, h].astype(F32) + wf[c, h, h]).astype(BF16)
         go(*w[c][2])
 
     def push_total(c):
@@ -350,20 +363,22 @@
     go(*q[1]["one"])
     take_all(*q[1]["y_in"])
     go(*q[1]["two"])
-    half(1, x, 0)
+    half(whole(1, x), 0)
     wo[1] = acc[...].reshape(wo.shape[1:])
     held[...] = tacc[...]
     take_all(*q[0]["one_in"])
     go(*q[0]["first"])
+    pair(0, y)
     take_all(*q[0]["two_in"])
     go(*q[0]["second"])
     x_total(pb, pu, pc, ps, p)
     go(*pg[0])
-    push_plus(0)
-    push_minus(0)
+    pair(0, 1 - y)
+    wb[0, xp, 1] = wf[0, 0, 1].astype(BF16)
+    wb[0, xm, 0] = wf[0, 1, 0].astype(BF16)
     take_all(*q[1]["one_in"])
     go(*q[1]["first"])
-    go(w[0][1][1])
+    go(*w[0][1])
     take_all(*q[1]["two_in"])
     go(*q[1]["second"])
     push_plus(1)
@@ -380,18 +395,19 @@
     unit(1, xo)
     go(t1[1], t1[0])
     push_halves(1)
-    positive = g_total(ps, pz, pg).astype(F32)
-    query = qa[:, x, y, z].reshape(ROWS, channels).astype(F32)
-    matched = jnp.sum(query * positive, axis=1, keepdims=True) / SOFTMAX_TEMP
     push_minus(1)
     go(t1[2])
     push_merged(0)
     go(w[1][1][1])
     acc[...] = wo[1].reshape(acc.shape)
     tacc[...] = held[...]
-    half(1, x, 1)
-    finish(1, x)
+    half(whole(1, x), 1)
+    finish(1, [(x, h) for h in range(NY)])
     wo[1] = acc[...].reshape(wo.shape[1:])
+
+    positive = g_total(ps, pz, pg).astype(F32)
+    query = qa[:, x, y, z].reshape(ROWS, channels).astype(F32)
+    matched = jnp.sum(query * positive, axis=1, keepdims=True) / SOFTMAX_TEMP
 
     take_all(tx, t1_in)
     total = ts[x]
@@ -412,6 +428,15 @@
     total = tg[0]
     for k in range(1, NG):
         total = total + tg[k]
+    logs = jnp.sum(jnp.log(total[: NY * CHUNKS]), axis=0, keepdims=True)
+    logs = jnp.sum(logs, axis=1, keepdims=True)
+    quarter = logs + NG * ROWS / SOFTMAX_TEMP - total[4:5, :1]
+    ms[spot] = jnp.broadcast_to(quarter, (8, 128))
+    m1_out, m1_in = channel(), channel()
+    rest = ms.at[pl.ds(0, NX * ND - 1)]
+    sent.append((rest, m1_out))
+    go(*[remote(ms.at[spot], ms.at[spot], peer, m1_out, m1_in) for peer in m_peers])
+
     lane = lax.broadcasted_iota(jnp.int32, (PART, HALF), 1)
     row = lax.broadcasted_iota(jnp.int32, (PART, HALF), 0)
     parts = []
@@ -420,15 +445,6 @@
         mine = jnp.where(lane == row + z * PART, jnp.broadcast_to(sums, (PART, HALF)), 0.0)
         parts.append(jnp.sum(mine, axis=1, keepdims=True))
     exponent_sum = jnp.concatenate(parts, axis=0)
-    logs = jnp.sum(jnp.log(total[: NY * CHUNKS]), axis=0, keepdims=True)
-    logs = jnp.sum(logs, axis=1, keepdims=True)
-    quarter = logs + NG * ROWS / SOFTMAX_TEMP - total[4:5, :1]
-    ms[spot] = jnp.broadcast_to(quarter, (8, 128))
-    m1_out, m1_in = channel(), channel()
-    rest = ms.at[pl.ds(0, NX * ND - 1)]
-    sent.append((rest, m1_out))
-    go(*[remote(ms.at[spot], ms.at[spot], peer, m1_out, m1_in) for peer in m_peers])
-
     loss = jnp.log(exponent_sum) + 1.0 / SOFTMAX_TEMP - matched
     diagonal = lax.broadcasted_iota(jnp.int32, (ROWS, ROWS), 0) == lax.broadcasted_iota(
         jnp.int32, (ROWS, ROWS), 1
@@ -485,7 +501,7 @@
         *chunked(rows=ROWS),
         vmem(BF16, CHUNKS, NX, NY, NZ, PART, channels),
         vmem(F32, ROWS, channels),
-        vmem(F32, CHUNKS, NY, HALF, channels),
+        vmem(F32, CHUNKS, 2, NY, HALF, channels),
         *chunked(CHUNKS, rows=PART)[:6],
         vmem(F32, CHUNKS, NY, NZ, PART, channels),
         vmem(BF16, CHUNKS, NG - 1, PART, channels),

time: 65 us -> 64.8 us (level)
  no operation moved by 1% of the time
where the time goes in v7:
time: 64.8 us; the launch traced here: 64.7 us
  Pallas kernels  61.7 us (95%)
  between operations  1.81 us (3%)
  local copies, waits for them, and re-layouts  1.13 us (2%)
    pallas_call x1, Pallas kernels, on_device(): pl.pallas_call(lambda *refs: kernel(count_all, *refs), out_shape=(pltpu.V...  61.7 us

profile of v7, /device:TPU:1, one launch (start us, length us, event | category | flops | bytes accessed | tf_op | source)
XLA Modules:
  0.0 64.7 jit_solution(14920869845289361956)
XLA Ops:
  0.6 61.7 %patch_nce.1 = (f32[1,32]{1,0:T(1,128)S(1)}, f32[32,256]{1,0:T(8,128)S(1)}, f32[1,128]{1,0:T(1,128)S(1)}) custom-call(s32[16,128]{1,0:T(8,128)} %refs_0_.1, s32[16,128]{1,0:T(8,128)} %bitcast.6, bf16[16,64,256]{2,1,0:T(8,128)(2,1)} %refs_2_.1, bf16[4096,256]{1,0:T(8,128)(2,1)} %refs_3_.1), custom_call_target="tpu_custom_call" | custom-call | tf_op jit(solution)/shard_map/patch_nce/pallas_call | solution.py:521
  62.4 0.5 copy.10
  62.9 0.6 copy.11
